TPU v7x, 256 devices: a whole 4x4x8 slice. The times are simulated.
256 devices in a mesh: grp: 8 (over x, core), ctx: 32 (over z, y).
Axes of the slice: x: 4, y: 4, z: 8, core: 2. Of those that a mesh axis runs over, the one named last changes fastest.
Arguments:
- queries: bfloat16 [32768, 4096], P(('grp', 'ctx')), parts along dimension 0, may hold values from -8 to 8
- key_states: bfloat16 [32768, 512], P(('grp', 'ctx')), parts along dimension 0, may hold values from -8 to 8
- value_states: bfloat16 [32768, 512], P(('grp', 'ctx')), parts along dimension 0, may hold values from -6 to 6
- grads_out: bfloat16 [32768, 4096], P(('grp', 'ctx')), parts along dimension 0, may hold values from -6 to 6
- doc_lengths: int32 [64], P('grp'), parts along dimension 0, may hold values from 1 to 1024, as said below
- block_plan: int32 [512], P('grp'), parts along dimension 0, may hold values from 0 to 63, as said below
- needed: int32 [256, 8], P('grp'), parts along dimension 0, may hold values from 0 to 63, as said below
Outputs:
- outputs: bfloat16 [32768, 4096], P(('grp', 'ctx')), parts along dimension 0
- query_grads: bfloat16 [32768, 4096], P(('grp', 'ctx')), parts along dimension 0
- key_grads: bfloat16 [32768, 512], P(('grp', 'ctx')), parts along dimension 0
- value_grads: bfloat16 [32768, 512], P(('grp', 'ctx')), parts along dimension 0
There are 8 independent parts, one for each index of `grp`. A program takes and returns all parts, laid end to end along the dimension named above; each array names one. Nothing has to cross between parts.
Inputs may be any that keep to these rules, and one draw needn't show every extreme that they name: `doc_lengths`: the lengths sum to 4096 and one of them is exactly 1024. `block_plan`: each block position appears once. `needed`: each row lists 8 different stored block numbers, no two of which have the same value of block number // 2.
All inputs are finite; a program needn't handle non-finite values.
Results may differ from a plain program's by a relative error of at most 0.013.
Values may be sent and summed in bfloat16 or wider, within the bound.
No kernel may reach another device: no remote copies, remote signals or barrier semaphores. Data moves between devices by JAX's collectives and lax.ppermute only.
A program may use at most 128 MiB of HBM per device.

v0:
```python
import math

import jax
import jax.numpy as jnp
from jax import lax
from jax.experimental import pallas as pl
from jax.experimental.pallas import tpu as pltpu
from jax.sharding import Mesh
from jax.sharding import PartitionSpec as P

HEADS = 32
KV_HEADS = 4
HEAD_DIM = 128
GROUP = HEADS // KV_HEADS
BLK = 64
NEED = 8
NDOC = 8
TOK = 128
ZN = 8
YN = 4
KVW = KV_HEADS * HEAD_DIM
KEYS = TOK + NEED * BLK
PAIR = 2 * TOK
SCALE = 1.0 / math.sqrt(HEAD_DIM)
LOG2E = math.log2(math.e)
HIDDEN = -1e30

FETCH = ((0, 1, -1, 2, -2), (3, -3, 4))
GIVE = ((3, -3), (2, -2, 4), (1, -1), (0,))
COLUMN = (0, 1, -1, 2, -2, 3, -3, 4)

VM = pl.BlockSpec(memory_space=pltpu.VMEM)
ANY = pl.BlockSpec(memory_space=pl.ANY)
FAR = pl.BlockSpec(memory_space=pltpu.HBM)
SM = pl.BlockSpec(memory_space=pltpu.SMEM)


def half(ref, part):
    return ref.at[pl.ds(pl.multiple_of(part * BLK, BLK), BLK), :]


def like(rows, cols=2 * KVW):
    return jax.ShapeDtypeStruct((rows, cols), jnp.bfloat16)


def listed(needed, rank, block):
    found = jnp.int32(0)
    for j in range(NEED):
        found = jnp.where(needed[j, rank] == block, 1, found)
    return found


def each_listed(needed, offsets, do):
    z, y = lax.axis_index("z"), lax.axis_index("y")
    for i, k in enumerate(offsets):
        owner = lax.rem(z + k + ZN, ZN) * YN + y
        for m in (1, 2, 3):
            rank = z * YN + lax.rem(y + m, YN)
            first, second = (listed(needed, rank, 2 * owner + p) for p in (0, 1))

            @pl.when(first + second > 0)
            def _(i=i, m=m, second=second):
                do(m, i, second)


def pack(needed, shards, offsets):
    count = len(offsets)

    def body(needed, *refs):
        ins, outs, sems = refs[:count], refs[count:-1], refs[-1]

        def copy(m, i, part):
            dst = outs[m - 1].at[pl.ds(i * BLK, BLK), :]
            return pltpu.make_async_copy(half(ins[i], part), dst, sems.at[i, m - 1])

        each_listed(needed, offsets, lambda *at: copy(*at).start())
        each_listed(needed, offsets, lambda *at: copy(*at).wait())

    return pl.pallas_call(
        body,
        out_shape=[like(count * BLK)] * 3,
        in_specs=[SM] + [ANY] * count,
        out_specs=[VM] * 3,
        scratch_shapes=[pltpu.SemaphoreType.DMA((count, 3))],
        name="pack",
    )(needed, *shards)


def shift(array, axis, size, by):
    return lax.ppermute(array, axis, [(i, (i + by) % size) for i in range(size)])


def to_mates(arrays, sign):
    return [shift(a, "y", YN, sign * m) for m, a in zip((1, 2, 3), arrays)]


def join(key_states, value_states):
    def body(k, v, kv):
        kv[:, :KVW] = k[...]
        kv[:, KVW:] = v[...]

    return pl.pallas_call(
        body,
        out_shape=like(TOK),
        in_specs=[VM, VM],
        out_specs=VM,
        name="join",
    )(key_states, value_states)


def gather(kv, needed):
    shards = {0: kv}
    shards[1], shards[-1] = shift(kv, "z", ZN, -1), shift(kv, "z", ZN, 1)
    shards[2], shards[-2] = shift(shards[1], "z", ZN, -1), shift(shards[-1], "z", ZN, 1)

    def packed(b):
        return pack(needed, [shards[k] for k in FETCH[b]], FETCH[b])

    mine = packed(0)
    first = to_mates(mine, 1)
    up, down, far, mine = lax.optimization_barrier((shards[2], shards[-2], kv, mine))
    shards[3], shards[-3] = shift(up, "z", ZN, -1), shift(down, "z", ZN, 1)
    shards[4] = shift(far, "z", ZN, 4)
    return shards, [first, to_mates(packed(1), 1)]


def attend_body(needed, plan, lengths, q_ref, do_ref, *refs):
    shards, refs = dict(zip(COLUMN, refs[:ZN])), refs[ZN:]
    received, refs = [refs[3 * b : 3 * b + 3] for b in range(len(FETCH))], refs[3 * len(FETCH) :]
    o_ref, dq_ref, grad_out, refs = refs[0], refs[1], refs[2], refs[3:]
    mate_out, refs = [refs[3 * b : 3 * b + 3] for b in range(len(GIVE))], refs[3 * len(GIVE) :]
    kv, grad, bias, table, qs, dos, pt, dst, sems = refs
    g = pl.program_id(0)
    z, y = lax.axis_index("z"), lax.axis_index("y")
    me = z * YN + y

    def slot_rows(j):
        return pl.ds(pl.multiple_of(TOK + j * BLK, BLK), BLK)

    def each_source(bundles, do):
        for b, offsets in enumerate(bundles):
            for i, k in enumerate(offsets):
                for m in range(YN):
                    j = table[m * ZN + k % ZN]

                    @pl.when(j >= 0)
                    def _(j=j, b=b, i=i, m=m, k=k):
                        do(j, b, i, m, k)

    @pl.when(g == 0)
    def _():
        own_copy = pltpu.make_async_copy(shards[0], kv.at[pl.ds(0, TOK), :], sems.at[NEED])
        own_copy.start()
        for i in range(YN * ZN):
            table[i] = -1
        for j in range(NEED):
            owner = needed[j, me] // 2
            distance = lax.rem(owner // YN - z + ZN, ZN)
            mate = lax.rem(y - lax.rem(owner, YN) + YN, YN)
            table[mate * ZN + distance] = j

        def fetch(j, b, i, m, k):
            if m == 0:
                src = half(shards[k], needed[j, me] % 2)
            else:
                src = received[b][m - 1].at[pl.ds(i * BLK, BLK), :]
            pltpu.make_async_copy(src, kv.at[slot_rows(j), :], sems.at[j]).start()

        each_source(FETCH, fetch)
        ends, total = [], jnp.int32(0)
        for d in range(NDOC):
            total = total + lengths[d]
            ends.append(total)

        def docs(place):
            found = jnp.zeros_like(place)
            for end in ends:
                found = found + (place >= end).astype(jnp.int32)
            return found

        lane = lax.broadcasted_iota(jnp.int32, (BLK, TOK), 1)
        first = lane < BLK
        q_place = jnp.where(first, plan[2 * me] * BLK, plan[2 * me + 1] * BLK) + lane % BLK
        q_doc = docs(q_place)
        row = lax.broadcasted_iota(jnp.int32, (BLK, TOK), 0)

        def block_bias(block, allowed):
            k_place = plan[block] * BLK + row
            seen = (docs(k_place) == q_doc) & (k_place <= q_place) & allowed
            return jnp.where(seen, 0.0, HIDDEN)

        for half_block in (0, 1):
            block = 2 * me + half_block
            also = listed(needed, me, block)
            same = (lane // BLK) == half_block
            bias[half_block * BLK : (half_block + 1) * BLK, :] = block_bias(
                block, same | ((row * 0 + also) == 1)
            )
        for j in range(NEED):
            block = needed[j, me]
            other = jnp.where(block // 2 == me, 0, 1)
            bias[TOK + j * BLK : TOK + (j + 1) * BLK, :] = block_bias(block, (row * 0 + other) == 1)
        own_copy.wait()
        for j in range(NEED):
            slot = kv.at[pl.ds(TOK + j * BLK, BLK), :]
            pltpu.make_async_copy(half(shards[0], 0), slot, sems.at[j]).wait()

    for h in range(GROUP):
        qs[h * TOK : (h + 1) * TOK, :] = q_ref[:, h * HEAD_DIM : (h + 1) * HEAD_DIM]
        dos[h * TOK : (h + 1) * TOK, :] = do_ref[:, h * HEAD_DIM : (h + 1) * HEAD_DIM]

    k_cols = pl.ds(pl.multiple_of(g * HEAD_DIM, HEAD_DIM), HEAD_DIM)
    v_cols = pl.ds(pl.multiple_of(KVW + g * HEAD_DIM, HEAD_DIM), HEAD_DIM)
    keys, values = kv[:, k_cols], kv[:, v_cols]
    wide_bias = jnp.concatenate([bias[...]] * 2, axis=1)

    def nt(a, b):
        return lax.dot_general(a, b, (((1,), (1,)), ((), ())), preferred_element_type=jnp.float32)

    def tn(a, b):
        return lax.dot_general(a, b, (((0,), (0,)), ((), ())), preferred_element_type=jnp.float32)

    def nn(a, b):
        return jnp.dot(a, b, preferred_element_type=jnp.float32)

    for pair in range(GROUP // 2):
        rows = slice(pair * PAIR, (pair + 1) * PAIR)
        scores = nt(keys, qs[rows, :]) * (SCALE * LOG2E) + wide_bias
        highest = jnp.max(scores, axis=0, keepdims=True)
        weights = jnp.exp2(scores - highest)
        weights = weights * (1.0 / jnp.sum(weights, axis=0, keepdims=True))
        low = weights.astype(jnp.bfloat16)
        pt[:, rows] = low
        prob_grads = nt(values, dos[rows, :])
        delta = jnp.sum(weights * prob_grads, axis=0, keepdims=True)
        score_grads = (weights * (prob_grads - delta)).astype(jnp.bfloat16)
        dst[:, rows] = score_grads
    out = tn(pt[...], values)
    dq = tn(dst[...], keys) * SCALE
    for h in range(GROUP):
        cols, rows = slice(h * HEAD_DIM, (h + 1) * HEAD_DIM), slice(h * TOK, (h + 1) * TOK)
        o_ref[:, cols] = out[rows, :].astype(jnp.bfloat16)
        dq_ref[:, cols] = dq[rows, :].astype(jnp.bfloat16)
    grad[:, k_cols] = (nn(dst[...], qs[...]) * SCALE).astype(jnp.bfloat16)
    grad[:, v_cols] = nn(pt[...], dos[...]).astype(jnp.bfloat16)

    @pl.when(g == KV_HEADS - 1)
    def _():
        whole = pltpu.make_async_copy(grad, grad_out, sems.at[NEED])
        whole.start()

        def send(j, b, i, m, k):
            if m > 0:
                target = mate_out[b][m - 1].at[pl.ds(i * BLK, BLK), :]
                pltpu.make_async_copy(grad.at[slot_rows(j), :], target, sems.at[j]).start()

        def sent(j, b, i, m, k):
            if m > 0:
                target = mate_out[b][m - 1].at[pl.ds(i * BLK, BLK), :]
                pltpu.make_async_copy(grad.at[slot_rows(j), :], target, sems.at[j]).wait()

        each_source(GIVE, send)
        each_source(GIVE, sent)
        whole.wait()


def attend(queries, grads_out, lengths, plan, needed, shards, received):
    block = pl.BlockSpec((TOK, GROUP * HEAD_DIM), lambda g: (0, g))
    ins = [shards[k] for k in COLUMN]
    for arrays in received:
        ins += arrays
    bf = jnp.bfloat16
    outs = [like(TOK, HEADS * HEAD_DIM)] * 2 + [like(KEYS)]
    for offsets in GIVE:
        outs += [like(len(offsets) * BLK)] * 3
    got = pl.pallas_call(
        attend_body,
        grid=(KV_HEADS,),
        out_shape=outs,
        in_specs=[SM] * 3 + [block] * 2 + [ANY] * len(ins),
        out_specs=[block] * 2 + [ANY] * (len(outs) - 2),
        scratch_shapes=[
            pltpu.VMEM((KEYS, 2 * KVW), bf),
            pltpu.VMEM((KEYS, 2 * KVW), bf),
            pltpu.VMEM((KEYS, TOK), jnp.float32),
            pltpu.SMEM((YN * ZN,), jnp.int32),
            pltpu.VMEM((GROUP * TOK, HEAD_DIM), bf),
            pltpu.VMEM((GROUP * TOK, HEAD_DIM), bf),
            pltpu.VMEM((KEYS, GROUP * TOK), bf),
            pltpu.VMEM((KEYS, GROUP * TOK), bf),
            pltpu.SemaphoreType.DMA((NEED + 1,)),
        ],
        compiler_params=pltpu.CompilerParams(vmem_limit_bytes=56 << 20),
        name="attend",
    )(needed, plan, lengths, queries, grads_out, *ins)
    return got[0], got[1], got[2], [got[3 + 3 * b : 6 + 3 * b] for b in range(len(GIVE))]


def combine(needed, grad, arrived, extra, offsets):
    n = len(offsets)
    home = offsets == (0,)

    def body(needed, grad, *refs):
        mates, refs = refs[:3], refs[3:]
        more, refs = refs[: len(extra)], refs[len(extra) :]
        outs, (acc, own, theirs, along, sems) = refs[:-5], refs[-5:]
        z, y = lax.axis_index("z"), lax.axis_index("y")
        me = z * YN + y

        def from_mate(m, i, part):
            src = mates[m - 1].at[pl.ds(i * BLK, BLK), :]
            return pltpu.make_async_copy(src, theirs.at[i, m - 1], sems.at[i, m])

        def own_slots(do):
            for i, k in enumerate(offsets):
                owner = lax.rem(z + k + ZN, ZN) * YN + y
                for j in range(NEED):

                    @pl.when(needed[j, me] // 2 == owner)
                    def _(i=i, j=j):
                        rows = pl.ds(TOK + j * BLK, BLK)
                        do(pltpu.make_async_copy(grad.at[rows, :], own.at[i], sems.at[i, 0]), i, j)

        ring = [
            pltpu.make_async_copy(r, along.at[e], sems.at[n, e]) for e, r in enumerate(more)
        ]
        for c in ring:
            c.start()
        each_listed(needed, offsets, lambda *at: from_mate(*at).start())
        if home:
            mine = pltpu.make_async_copy(grad.at[pl.ds(0, TOK), :], own, sems.at[0, 0])
            mine.start()
            mine.wait()
            acc[0] = own[...].astype(jnp.float32)
        else:
            own_slots(lambda c, i, j: c.start())
            if not ring:
                acc[...] = jnp.zeros_like(acc)
        for e, c in enumerate(ring):
            c.wait()
            if home:
                acc[0] += along[e].astype(jnp.float32)
            else:
                acc[e] = along[e].astype(jnp.float32)
        if n > len(ring) and ring:
            acc[n - 1] = jnp.zeros((TOK, 2 * KVW), jnp.float32)

        def add_mate(m, i, part):
            from_mate(m, i, part).wait()
            half(acc.at[i], part)[...] += theirs[i, m - 1].astype(jnp.float32)

        def add_own(c, i, j):
            c.wait()
            half(acc.at[i], needed[j, me] % 2)[...] += own[i].astype(jnp.float32)

        each_listed(needed, offsets, add_mate)
        if home:
            outs[0][...] = acc[0, :, :KVW].astype(jnp.bfloat16)
            outs[1][...] = acc[0, :, KVW:].astype(jnp.bfloat16)
        else:
            own_slots(add_own)
            for i in range(n):
                outs[i][...] = acc[i].astype(jnp.bfloat16)

    shapes = [like(TOK, KVW)] * 2 if home else [like(TOK)] * n
    return pl.pallas_call(
        body,
        out_shape=shapes,
        in_specs=[SM, FAR] + [ANY] * (3 + len(extra)),
        out_specs=[VM] * len(shapes),
        scratch_shapes=[
            pltpu.VMEM((n, TOK, 2 * KVW), jnp.float32),
            pltpu.VMEM((TOK, 2 * KVW) if home else (n, BLK, 2 * KVW), jnp.bfloat16),
            pltpu.VMEM((n, 3, BLK, 2 * KVW), jnp.bfloat16),
            pltpu.VMEM((max(len(extra), 1), TOK, 2 * KVW), jnp.bfloat16),
            pltpu.SemaphoreType.DMA((n + 1, YN)),
        ],
        compiler_params=pltpu.CompilerParams(vmem_limit_bytes=16 << 20),
        name="combine",
    )(needed, grad, *arrived, *extra)


def scatter(grad, mates, needed):
    def hop(arrays):
        return [shift(arrays[0], "z", ZN, 1), shift(arrays[1], "z", ZN, -1)]

    third = to_mates(mates[0], -1)
    second = to_mates(mates[1], -1)
    ring = list(combine(needed, grad, third, [], GIVE[0]))
    first, last, ring[0] = lax.optimization_barrier((mates[2], mates[3], ring[0]))
    first = to_mates(first, -1)
    ring = hop(ring)
    up, down, far = combine(needed, grad, second, ring, GIVE[1])
    last, up = lax.optimization_barrier((last, up))
    far = shift(far, "z", ZN, 4)
    ring = hop([up, down])
    last = to_mates(last, -1)
    ring = hop(combine(needed, grad, first, ring, GIVE[2]))
    return combine(needed, grad, last, ring + [far], GIVE[3])


def on_device(queries, key_states, value_states, grads_out, lengths, plan, needed):
    needed = needed.T
    shards, received = gather(join(key_states, value_states), needed)
    outputs, query_grads, grad, mates = attend(
        queries, grads_out, lengths, plan, needed, shards, received
    )
    key_grads, value_grads = scatter(grad, mates, needed)
    return outputs, query_grads, key_grads, value_grads


def solution(mesh):
    torus = Mesh(mesh.devices.reshape(mesh.shape["grp"], ZN, YN), ("grp", "z", "y"))
    rows = P(("grp", "z", "y"), None)
    return jax.shard_map(
        on_device,
        mesh=torus,
        in_specs=(rows, rows, rows, rows, P("grp"), P("grp"), P("grp", None)),
        out_specs=(rows, rows, rows, rows),
        check_vma=False,
    )
```

profile of v0, /device:TPU:4, one launch (start us, length us, event | category | flops | bytes accessed | tf_op | source)
XLA Modules:
  0.0 174.2 jit_solution(17288869664061351329)
XLA Ops:
  0.6 1.7 join.1.refs_0_
  2.3 1.9 %collective-permute-start.1 = (bf16[128,1024]{1,0:T(8,128)(2,1)}, bf16[128,1024]{1,0:T(8,128)(2,1)S(1)}, u32[]{:S(2)}, u32[]{:S(2)}) collective-permute-start(bf16[128,1024]{1,0:T(8,128)(2,1)} %join.1.refs_0_), channel_id=1, source_target_pairs={{0,4},{4,8},{8,12},{12,16},{16,20},{20,24},{24,28},{28,0},{1,5},{5... | collective-permute-start | bytes 786440 | tf_op jit(solution)/shard_map/ppermute | solution.py:90
  4.3 3.9 %collective-permute-start = (bf16[128,1024]{1,0:T(8,128)(2,1)}, bf16[128,1024]{1,0:T(8,128)(2,1)S(1)}, u32[]{:S(2)}, u32[]{:S(2)}) collective-permute-start(bf16[128,1024]{1,0:T(8,128)(2,1)} %join.1.refs_0_), channel_id=1, source_target_pairs={{0,28},{4,0},{8,4},{12,8},{16,12},{20,16},{24,20},{28,24},{1,29},{... | collective-permute-start | bytes 786440 | tf_op jit(solution)/shard_map/ppermute | solution.py:90
  8.2 6.6 %collective-permute-done.1.refs_2_ = bf16[128,1024]{1,0:T(8,128)(2,1)S(1)} collective-permute-done((bf16[128,1024]{1,0:T(8,128)(2,1)}, bf16[128,1024]{1,0:T(8,128)(2,1)S(1)}, u32[]{:S(2)}, u32[]{:S(2)}) %collective-permute-start.1) | collective-permute-done | bytes 262176 | tf_op jit(solution)/shard_map/ppermute | solution.py:90
  14.8 3.2 %collective-permute-start.2 = (bf16[128,1024]{1,0:T(8,128)(2,1)S(1)}, bf16[128,1024]{1,0:T(8,128)(2,1)S(1)}, u32[]{:S(2)}, u32[]{:S(2)}) collective-permute-start(bf16[128,1024]{1,0:T(8,128)(2,1)S(1)} %collective-permute-done.refs_1_), channel_id=1, source_target_pairs={{0,28},{4,0},{8,4},{12,8},{16,12},{20,16},{24,20},{28,24},{1,29},{... | collective-permute-start | bytes 786440 | tf_op jit(solution)/shard_map/ppermute | solution.py:90
  18.0 5.5 %collective-permute-done.3.refs_4_ = bf16[128,1024]{1,0:T(8,128)(2,1)S(1)} collective-permute-done((bf16[128,1024]{1,0:T(8,128)(2,1)S(1)}, bf16[128,1024]{1,0:T(8,128)(2,1)S(1)}, u32[]{:S(2)}, u32[]{:S(2)}) %collective-permute-start.3) | collective-permute-done | bytes 262176 | tf_op jit(solution)/shard_map/ppermute | solution.py:90
  24.3 3.4 %pack.2 = (bf16[320,1024]{1,0:T(8,128)(2,1)}, bf16[320,1024]{1,0:T(8,128)(2,1)}, bf16[320,1024]{1,0:T(8,128)(2,1)}) custom-call(s32[8,32]{1,0:T(8,128)} %bitcast.1, bf16[128,1024]{1,0:T(8,128)(2,1)} %join.1.refs_0_, bf16[128,1024]{1,0:T(8,128)(2,1)} %copy-done.4, bf16[128,1024]{1,0:T(8,128)(2,1)} %copy-done.3, bf16[128,1024]{1,0:T(8,128)(2,1)} %copy-done.6, ...), custom_call_target="tpu_custom_call" | custom-call | tf_op jit(solution)/shard_map/pack/pallas_call | solution.py:79
  27.7 1.8 %collective-permute-start.7 = (bf16[320,1024]{1,0:T(8,128)(2,1)}, bf16[320,1024]{1,0:T(8,128)(2,1)S(1)}, u32[]{:S(2)}, u32[]{:S(2)}) collective-permute-start(bf16[320,1024]{1,0:T(8,128)(2,1)} %get-tuple-element.48), channel_id=1, source_target_pairs={{0,1},{1,2},{2,3},{3,0},{4,5},{5,6},{6,7},{7,4},{8,9},{9,10},{10,1... | collective-permute-start | bytes 1966088 | tf_op jit(solution)/shard_map/ppermute | solution.py:90
  29.5 2.7 %collective-permute-start.4 = (bf16[128,1024]{1,0:T(8,128)(2,1)}, bf16[128,1024]{1,0:T(8,128)(2,1)S(1)}, u32[]{:S(2)}, u32[]{:S(2)}) collective-permute-start(bf16[128,1024]{1,0:T(8,128)(2,1)} %copy-done.6), channel_id=1, source_target_pairs={{0,28},{4,0},{8,4},{12,8},{16,12},{20,16},{24,20},{28,24},{1,29},{... | collective-permute-start | bytes 786440 | tf_op jit(solution)/shard_map/ppermute | solution.py:90
  32.1 3.9 %collective-permute-start.6 = (bf16[128,1024]{1,0:T(8,128)(2,1)S(1)}, bf16[128,1024]{1,0:T(8,128)(2,1)S(1)}, u32[]{:S(2)}, u32[]{:S(2)}) collective-permute-start(bf16[128,1024]{1,0:T(8,128)(2,1)S(1)} %copy-done.2), channel_id=1, source_target_pairs={{0,16},{4,20},{8,24},{12,28},{16,0},{20,4},{24,8},{28,12},{1,17},{... | collective-permute-start | bytes 786440 | tf_op jit(solution)/shard_map/ppermute | solution.py:90
  36.0 3.0 %collective-permute-start.8 = (bf16[320,1024]{1,0:T(8,128)(2,1)}, bf16[320,1024]{1,0:T(8,128)(2,1)S(1)}, u32[]{:S(2)}, u32[]{:S(2)}) collective-permute-start(bf16[320,1024]{1,0:T(8,128)(2,1)} %get-tuple-element.49), channel_id=1, source_target_pairs={{0,2},{1,3},{2,0},{3,1},{4,6},{5,7},{6,4},{7,5},{8,10},{9,11},{10,... | collective-permute-start | bytes 1966088 | tf_op jit(solution)/shard_map/ppermute | solution.py:90
  39.0 6.3 %collective-permute-done.4.refs_0_.refs_5_ = bf16[128,1024]{1,0:T(8,128)(2,1)S(1)} collective-permute-done((bf16[128,1024]{1,0:T(8,128)(2,1)}, bf16[128,1024]{1,0:T(8,128)(2,1)S(1)}, u32[]{:S(2)}, u32[]{:S(2)}) %collective-permute-start.4) | collective-permute-done | bytes 262176 | tf_op jit(solution)/shard_map/ppermute | solution.py:90
  45.3 1.5 collective-permute-start.9
  46.7 2.7 %collective-permute-done.5.refs_1_.refs_6_ = bf16[128,1024]{1,0:T(8,128)(2,1)S(1)} collective-permute-done((bf16[128,1024]{1,0:T(8,128)(2,1)}, bf16[128,1024]{1,0:T(8,128)(2,1)S(1)}, u32[]{:S(2)}, u32[]{:S(2)}) %collective-permute-start.5) | collective-permute-done | bytes 262176 | tf_op jit(solution)/shard_map/ppermute | solution.py:90
  49.5 1.8 %collective-permute-done.6.refs_2_.refs_7_ = bf16[128,1024]{1,0:T(8,128)(2,1)S(1)} collective-permute-done((bf16[128,1024]{1,0:T(8,128)(2,1)S(1)}, bf16[128,1024]{1,0:T(8,128)(2,1)S(1)}, u32[]{:S(2)}, u32[]{:S(2)}) %collective-permute-start.6) | collective-permute-done | bytes 262176 | tf_op jit(solution)/shard_map/ppermute | solution.py:90
  52.0 2.9 %pack.3 = (bf16[192,1024]{1,0:T(8,128)(2,1)}, bf16[192,1024]{1,0:T(8,128)(2,1)}, bf16[192,1024]{1,0:T(8,128)(2,1)}) custom-call(s32[8,32]{1,0:T(8,128)} %bitcast.2, bf16[128,1024]{1,0:T(8,128)(2,1)} %copy-done.7, bf16[128,1024]{1,0:T(8,128)(2,1)} %copy-done.8, bf16[128,1024]{1,0:T(8,128)(2,1)} %copy-done.9), custom_call_target="tpu_custom_call" | custom-call | tf_op jit(solution)/shard_map/pack/pallas_call | solution.py:79
  54.9 1.8 %collective-permute-start.10 = (bf16[192,1024]{1,0:T(8,128)(2,1)}, bf16[192,1024]{1,0:T(8,128)(2,1)S(1)}, u32[]{:S(2)}, u32[]{:S(2)}) collective-permute-start(bf16[192,1024]{1,0:T(8,128)(2,1)} %get-tuple-element.54), channel_id=1, source_target_pairs={{0,1},{1,2},{2,3},{3,0},{4,5},{5,6},{6,7},{7,4},{8,9},{9,10},{10,1... | collective-permute-start | bytes 1179656 | tf_op jit(solution)/shard_map/ppermute | solution.py:90
  56.7 1.8 %collective-permute-start.11 = (bf16[192,1024]{1,0:T(8,128)(2,1)}, bf16[192,1024]{1,0:T(8,128)(2,1)S(1)}, u32[]{:S(2)}, u32[]{:S(2)}) collective-permute-start(bf16[192,1024]{1,0:T(8,128)(2,1)} %get-tuple-element.55), channel_id=1, source_target_pairs={{0,2},{1,3},{2,0},{3,1},{4,6},{5,7},{6,4},{7,5},{8,10},{9,11},{10,... | collective-permute-start | bytes 1179656 | tf_op jit(solution)/shard_map/ppermute | solution.py:90
  58.5 2.0 %collective-permute-start.12 = (bf16[192,1024]{1,0:T(8,128)(2,1)}, bf16[192,1024]{1,0:T(8,128)(2,1)S(1)}, u32[]{:S(2)}, u32[]{:S(2)}) collective-permute-start(bf16[192,1024]{1,0:T(8,128)(2,1)} %get-tuple-element.56), channel_id=1, source_target_pairs={{0,3},{1,0},{2,1},{3,2},{4,7},{5,4},{6,5},{7,6},{8,11},{9,8},{10,9... | collective-permute-start | bytes 1179656 | tf_op jit(solution)/shard_map/ppermute | solution.py:90
  61.4 8.8 %collective-permute-done.9.refs_10_ = bf16[320,1024]{1,0:T(8,128)(2,1)S(1)} collective-permute-done((bf16[320,1024]{1,0:T(8,128)(2,1)}, bf16[320,1024]{1,0:T(8,128)(2,1)S(1)}, u32[]{:S(2)}, u32[]{:S(2)}) %collective-permute-start.9) | collective-permute-done | bytes 655392 | tf_op jit(solution)/shard_map/ppermute | solution.py:90
  70.2 6.1 %collective-permute-done.11.refs_12_ = bf16[192,1024]{1,0:T(8,128)(2,1)S(1)} collective-permute-done((bf16[192,1024]{1,0:T(8,128)(2,1)}, bf16[192,1024]{1,0:T(8,128)(2,1)S(1)}, u32[]{:S(2)}, u32[]{:S(2)}) %collective-permute-start.11) | collective-permute-done | bytes 393248 | tf_op jit(solution)/shard_map/ppermute | solution.py:90
  76.3 5.2 %collective-permute-done.12.refs_13_ = bf16[192,1024]{1,0:T(8,128)(2,1)S(1)} collective-permute-done((bf16[192,1024]{1,0:T(8,128)(2,1)}, bf16[192,1024]{1,0:T(8,128)(2,1)S(1)}, u32[]{:S(2)}, u32[]{:S(2)}) %collective-permute-start.12) | collective-permute-done | bytes 393248 | tf_op jit(solution)/shard_map/ppermute | solution.py:90
  82.3 17.4 %attend.1 = (bf16[128,4096]{1,0:T(8,128)(2,1)}, bf16[128,4096]{1,0:T(8,128)(2,1)}, bf16[640,1024]{1,0:T(8,128)(2,1)}, bf16[128,1024]{1,0:T(8,128)(2,1)}, bf16[12...) custom-call(s32[8,32]{1,0:T(8,128)} %bitcast.3, ...), custom_call_target="tpu_custom_call" | custom-call | tf_op jit(solution)/shard_map/attend/pallas_call | solution.py:276
  99.7 2.7 %collective-permute-start.13 = (bf16[128,1024]{1,0:T(8,128)(2,1)}, bf16[128,1024]{1,0:T(8,128)(2,1)S(1)}, u32[]{:S(2)}, u32[]{:S(2)}) collective-permute-start(bf16[128,1024]{1,0:T(8,128)(2,1)} %get-tuple-element.66), channel_id=1, source_target_pairs={{0,3},{1,0},{2,1},{3,2},{4,7},{5,4},{6,5},{7,6},{8,11},{9,8},{10,9... | collective-permute-start | bytes 786440 | tf_op jit(solution)/shard_map/ppermute | solution.py:90
  102.3 1.0 collective-permute-start.14
  104.1 2.5 %collective-permute-start.16 = (bf16[192,1024]{1,0:T(8,128)(2,1)}, bf16[192,1024]{1,0:T(8,128)(2,1)S(1)}, u32[]{:S(2)}, u32[]{:S(2)}) collective-permute-start(bf16[192,1024]{1,0:T(8,128)(2,1)} %get-tuple-element.73), channel_id=1, source_target_pairs={{0,3},{1,0},{2,1},{3,2},{4,7},{5,4},{6,5},{7,6},{8,11},{9,8},{10,9... | collective-permute-start | bytes 1179656 | tf_op jit(solution)/shard_map/ppermute | solution.py:90
  106.6 1.3 collective-permute-start.17
  107.9 6.9 %collective-permute-done.13.refs_0_ = bf16[128,1024]{1,0:T(8,128)(2,1)S(1)} collective-permute-done((bf16[128,1024]{1,0:T(8,128)(2,1)}, bf16[128,1024]{1,0:T(8,128)(2,1)S(1)}, u32[]{:S(2)}, u32[]{:S(2)}) %collective-permute-start.13) | collective-permute-done | bytes 262176 | tf_op jit(solution)/shard_map/ppermute | solution.py:90
  115.5 6.8 %collective-permute-done.15.refs_2_ = bf16[128,1024]{1,0:T(8,128)(2,1)S(1)} collective-permute-done((bf16[128,1024]{1,0:T(8,128)(2,1)}, bf16[128,1024]{1,0:T(8,128)(2,1)S(1)}, u32[]{:S(2)}, u32[]{:S(2)}) %collective-permute-start.15) | collective-permute-done | bytes 262176 | tf_op jit(solution)/shard_map/ppermute | solution.py:90
  122.4 1.3 copy-done
  123.7 1.6 combine.4
  125.4 4.0 %collective-permute-start.20 = (bf16[128,1024]{1,0:T(8,128)(2,1)S(1)}, bf16[128,1024]{1,0:T(8,128)(2,1)S(1)}, u32[]{:S(2)}, u32[]{:S(2)}) collective-permute-start(bf16[128,1024]{1,0:T(8,128)(2,1)S(1)} %get-tuple-element.77), channel_id=1, source_target_pairs={{0,28},{4,0},{8,4},{12,8},{16,12},{20,16},{24,20},{28,24},{1,29},{... | collective-permute-start | bytes 786440 | tf_op jit(solution)/shard_map/ppermute | solution.py:90
  129.4 1.0 collective-permute-done.16.refs_0_
  130.4 3.7 %collective-permute-start.24 = (bf16[128,1024]{1,0:T(8,128)(2,1)S(1)}, bf16[128,1024]{1,0:T(8,128)(2,1)S(1)}, u32[]{:S(2)}, u32[]{:S(2)}) collective-permute-start(bf16[128,1024]{1,0:T(8,128)(2,1)S(1)} %copy-done.18), channel_id=1, source_target_pairs={{0,3},{1,0},{2,1},{3,2},{4,7},{5,4},{6,5},{7,6},{8,11},{9,8},{10,9... | collective-permute-start | bytes 786440 | tf_op jit(solution)/shard_map/ppermute | solution.py:90
  134.2 1.5 collective-permute-done.18.refs_2_
  135.7 2.6 %combine.5 = (bf16[128,1024]{1,0:T(8,128)(2,1)S(1)}, bf16[128,1024]{1,0:T(8,128)(2,1)S(1)}, bf16[128,1024]{1,0:T(8,128)(2,1)S(1)}) custom-call(s32[8,32]{1,0:T(8,128)S(1)} %bitcast.5, bf16[640,1024]{1,0:T(8,128)(2,1)S(1)} %copy-done, bf16[192,1024]{1,0:T(8,128)(2,1)S(1)} %collective-permute-done.16.refs_0_, ...), custom_call_target="tpu_custom_call" | custom-call | tf_op jit(solution)/shard_map/combine/pallas_call | solution.py:366
  138.4 3.8 %collective-permute-start.28 = (bf16[128,1024]{1,0:T(8,128)(2,1)S(1)}, bf16[128,1024]{1,0:T(8,128)(2,1)S(1)}, u32[]{:S(2)}, u32[]{:S(2)}) collective-permute-start(bf16[128,1024]{1,0:T(8,128)(2,1)S(1)} %get-tuple-element.86), channel_id=1, source_target_pairs={{0,28},{4,0},{8,4},{12,8},{16,12},{20,16},{24,20},{28,24},{1,29},{... | collective-permute-start | bytes 786440 | tf_op jit(solution)/shard_map/ppermute | solution.py:90
  142.2 2.4 %collective-permute-start.21 = (bf16[64,1024]{1,0:T(8,128)(2,1)S(1)}, bf16[64,1024]{1,0:T(8,128)(2,1)S(1)}, u32[]{:S(2)}, u32[]{:S(2)}) collective-permute-start(bf16[64,1024]{1,0:T(8,128)(2,1)S(1)} %copy-done.21), channel_id=1, source_target_pairs={{0,3},{1,0},{2,1},{3,2},{4,7},{5,4},{6,5},{7,6},{8,11},{9,8},{10,9... | collective-permute-start | bytes 393224 | tf_op jit(solution)/shard_map/ppermute | solution.py:90
  144.6 1.2 collective-permute-start.31
  145.8 1.9 %collective-permute-done.26.refs_2_ = bf16[128,1024]{1,0:T(8,128)(2,1)S(1)} collective-permute-done((bf16[128,1024]{1,0:T(8,128)(2,1)S(1)}, bf16[128,1024]{1,0:T(8,128)(2,1)S(1)}, u32[]{:S(2)}, u32[]{:S(2)}) %collective-permute-start.26) | collective-permute-done | bytes 262176 | tf_op jit(solution)/shard_map/ppermute | solution.py:90
  147.7 8.5 %collective-permute-done.28.refs_4_ = bf16[128,1024]{1,0:T(8,128)(2,1)S(1)} collective-permute-done((bf16[128,1024]{1,0:T(8,128)(2,1)S(1)}, bf16[128,1024]{1,0:T(8,128)(2,1)S(1)}, u32[]{:S(2)}, u32[]{:S(2)}) %collective-permute-start.28) | collective-permute-done | bytes 262176 | tf_op jit(solution)/shard_map/ppermute | solution.py:90
  156.2 1.6 combine.6
  157.9 4.9 %collective-permute-start.30 = (bf16[128,1024]{1,0:T(8,128)(2,1)S(1)}, bf16[128,1024]{1,0:T(8,128)(2,1)S(1)}, u32[]{:S(2)}, u32[]{:S(2)}) collective-permute-start(bf16[128,1024]{1,0:T(8,128)(2,1)S(1)} %get-tuple-element.88), channel_id=1, source_target_pairs={{0,28},{4,0},{8,4},{12,8},{16,12},{20,16},{24,20},{28,24},{1,29},{... | collective-permute-start | bytes 786440 | tf_op jit(solution)/shard_map/ppermute | solution.py:90
  162.8 3.1 %collective-permute-start.22 = (bf16[64,1024]{1,0:T(8,128)(2,1)S(1)}, bf16[64,1024]{1,0:T(8,128)(2,1)S(1)}, u32[]{:S(2)}, u32[]{:S(2)}) collective-permute-start(bf16[64,1024]{1,0:T(8,128)(2,1)S(1)} %copy-done.20), channel_id=1, source_target_pairs={{0,2},{1,3},{2,0},{3,1},{4,6},{5,7},{6,4},{7,5},{8,10},{9,11},{10,... | collective-permute-start | bytes 393224 | tf_op jit(solution)/shard_map/ppermute | solution.py:90
  165.9 2.2 %collective-permute-start.23 = (bf16[64,1024]{1,0:T(8,128)(2,1)S(1)}, bf16[64,1024]{1,0:T(8,128)(2,1)S(1)}, u32[]{:S(2)}, u32[]{:S(2)}) collective-permute-start(bf16[64,1024]{1,0:T(8,128)(2,1)S(1)} %copy-done.19), channel_id=1, source_target_pairs={{0,1},{1,2},{2,3},{3,0},{4,5},{5,6},{6,7},{7,4},{8,9},{9,10},{10,1... | collective-permute-start | bytes 393224 | tf_op jit(solution)/shard_map/ppermute | solution.py:90
  168.1 2.4 %collective-permute-done.22.refs_1_ = bf16[64,1024]{1,0:T(8,128)(2,1)S(1)} collective-permute-done((bf16[64,1024]{1,0:T(8,128)(2,1)S(1)}, bf16[64,1024]{1,0:T(8,128)(2,1)S(1)}, u32[]{:S(2)}, u32[]{:S(2)}) %collective-permute-start.22) | collective-permute-done | bytes 131104 | tf_op jit(solution)/shard_map/ppermute | solution.py:90
  170.5 1.6 collective-permute-done.23.refs_2_
  172.1 2.0 %combine.7 = (bf16[128,512]{1,0:T(8,128)(2,1)}, bf16[128,512]{1,0:T(8,128)(2,1)}) custom-call(s32[8,32]{1,0:T(8,128)S(1)} %bitcast.7, bf16[640,1024]{1,0:T(8,128)(2,1)S(1)} %copy-done, bf16[64,1024]{1,0:T(8,128)(2,1)S(1)} %collective-permute-done.21.refs_0_, bf16[64,1024]{1,0:T(8,128)(2,1)S(1)} %collective-permute-done.22.refs_1_, ...), custom_call_target="tpu_custom_call" | custom-call | tf_op jit(solution)/shard_map/combine/pallas_call | solution.py:366
  (68 shorter events, 5.1 us)
Async XLA Ops:
  2.3 29.8 %copy-start.2 = (bf16[128,1024]{1,0:T(8,128)(2,1)S(1)}, bf16[128,1024]{1,0:T(8,128)(2,1)}, u32[]{:S(2)}) copy-start(bf16[128,1024]{1,0:T(8,128)(2,1)} %join.1.refs_0_) | copy-start | bytes 786436
  2.3 12.4 %collective-permute-start.1 = (bf16[128,1024]{1,0:T(8,128)(2,1)}, bf16[128,1024]{1,0:T(8,128)(2,1)S(1)}, u32[]{:S(2)}, u32[]{:S(2)}) collective-permute-start(bf16[128,1024]{1,0:T(8,128)(2,1)} %join.1.refs_0_), channel_id=1, source_target_pairs={{0,4},{4,8},{8,12},{12,16},{16,20},{20,24},{24,28},{28,0},{1,5},{5... | collective-permute-start | bytes 786440 | tf_op jit(solution)/shard_map/ppermute | solution.py:90
  4.3 10.5 %collective-permute-start = (bf16[128,1024]{1,0:T(8,128)(2,1)}, bf16[128,1024]{1,0:T(8,128)(2,1)S(1)}, u32[]{:S(2)}, u32[]{:S(2)}) collective-permute-start(bf16[128,1024]{1,0:T(8,128)(2,1)} %join.1.refs_0_), channel_id=1, source_target_pairs={{0,28},{4,0},{8,4},{12,8},{16,12},{20,16},{24,20},{28,24},{1,29},{... | collective-permute-start | bytes 786440 | tf_op jit(solution)/shard_map/ppermute | solution.py:90
  14.8 8.7 %copy-start.3 = (bf16[128,1024]{1,0:T(8,128)(2,1)}, bf16[128,1024]{1,0:T(8,128)(2,1)S(1)}, u32[]{:S(2)}) copy-start(bf16[128,1024]{1,0:T(8,128)(2,1)S(1)} %collective-permute-done.1.refs_2_) | copy-start | bytes 786436
  14.8 8.7 %collective-permute-start.3 = (bf16[128,1024]{1,0:T(8,128)(2,1)S(1)}, bf16[128,1024]{1,0:T(8,128)(2,1)S(1)}, u32[]{:S(2)}, u32[]{:S(2)}) collective-permute-start(bf16[128,1024]{1,0:T(8,128)(2,1)S(1)} %collective-permute-done.1.refs_2_), channel_id=1, source_target_pairs={{0,4},{4,8},{8,12},{12,16},{16,20},{20,24},{24,28},{28,0},{1,5},{5... | collective-permute-start | bytes 786440 | tf_op jit(solution)/shard_map/ppermute | solution.py:90
  14.8 8.7 %copy-start.4 = (bf16[128,1024]{1,0:T(8,128)(2,1)}, bf16[128,1024]{1,0:T(8,128)(2,1)S(1)}, u32[]{:S(2)}) copy-start(bf16[128,1024]{1,0:T(8,128)(2,1)S(1)} %collective-permute-done.refs_1_) | copy-start | bytes 786436
  14.8 8.7 %collective-permute-start.2 = (bf16[128,1024]{1,0:T(8,128)(2,1)S(1)}, bf16[128,1024]{1,0:T(8,128)(2,1)S(1)}, u32[]{:S(2)}, u32[]{:S(2)}) collective-permute-start(bf16[128,1024]{1,0:T(8,128)(2,1)S(1)} %collective-permute-done.refs_1_), channel_id=1, source_target_pairs={{0,28},{4,0},{8,4},{12,8},{16,12},{20,16},{24,20},{28,24},{1,29},{... | collective-permute-start | bytes 786440 | tf_op jit(solution)/shard_map/ppermute | solution.py:90
  27.7 30.8 %collective-permute-start.7 = (bf16[320,1024]{1,0:T(8,128)(2,1)}, bf16[320,1024]{1,0:T(8,128)(2,1)S(1)}, u32[]{:S(2)}, u32[]{:S(2)}) collective-permute-start(bf16[320,1024]{1,0:T(8,128)(2,1)} %get-tuple-element.48), channel_id=1, source_target_pairs={{0,1},{1,2},{2,3},{3,0},{4,5},{5,6},{6,7},{7,4},{8,9},{9,10},{10,1... | collective-permute-start | bytes 1966088 | tf_op jit(solution)/shard_map/ppermute | solution.py:90
  29.5 15.8 %collective-permute-start.4 = (bf16[128,1024]{1,0:T(8,128)(2,1)}, bf16[128,1024]{1,0:T(8,128)(2,1)S(1)}, u32[]{:S(2)}, u32[]{:S(2)}) collective-permute-start(bf16[128,1024]{1,0:T(8,128)(2,1)} %copy-done.6), channel_id=1, source_target_pairs={{0,28},{4,0},{8,4},{12,8},{16,12},{20,16},{24,20},{28,24},{1,29},{... | collective-permute-start | bytes 786440 | tf_op jit(solution)/shard_map/ppermute | solution.py:90
  32.1 17.3 %collective-permute-start.5 = (bf16[128,1024]{1,0:T(8,128)(2,1)}, bf16[128,1024]{1,0:T(8,128)(2,1)S(1)}, u32[]{:S(2)}, u32[]{:S(2)}) collective-permute-start(bf16[128,1024]{1,0:T(8,128)(2,1)} %copy-done.5), channel_id=1, source_target_pairs={{0,4},{4,8},{8,12},{12,16},{16,20},{20,24},{24,28},{28,0},{1,5},{5... | collective-permute-start | bytes 786440 | tf_op jit(solution)/shard_map/ppermute | solution.py:90
  32.1 19.1 %collective-permute-start.6 = (bf16[128,1024]{1,0:T(8,128)(2,1)S(1)}, bf16[128,1024]{1,0:T(8,128)(2,1)S(1)}, u32[]{:S(2)}, u32[]{:S(2)}) collective-permute-start(bf16[128,1024]{1,0:T(8,128)(2,1)S(1)} %copy-done.2), channel_id=1, source_target_pairs={{0,16},{4,20},{8,24},{12,28},{16,0},{20,4},{24,8},{28,12},{1,17},{... | collective-permute-start | bytes 786440 | tf_op jit(solution)/shard_map/ppermute | solution.py:90
  36.0 25.4 %collective-permute-start.8 = (bf16[320,1024]{1,0:T(8,128)(2,1)}, bf16[320,1024]{1,0:T(8,128)(2,1)S(1)}, u32[]{:S(2)}, u32[]{:S(2)}) collective-permute-start(bf16[320,1024]{1,0:T(8,128)(2,1)} %get-tuple-element.49), channel_id=1, source_target_pairs={{0,2},{1,3},{2,0},{3,1},{4,6},{5,7},{6,4},{7,5},{8,10},{9,11},{10,... | collective-permute-start | bytes 1966088 | tf_op jit(solution)/shard_map/ppermute | solution.py:90
  45.3 6.0 %copy-start.7 = (bf16[128,1024]{1,0:T(8,128)(2,1)}, bf16[128,1024]{1,0:T(8,128)(2,1)S(1)}, u32[]{:S(2)}) copy-start(bf16[128,1024]{1,0:T(8,128)(2,1)S(1)} %collective-permute-done.4.refs_0_.refs_5_) | copy-start | bytes 786436
  45.3 24.9 %collective-permute-start.9 = (bf16[320,1024]{1,0:T(8,128)(2,1)}, bf16[320,1024]{1,0:T(8,128)(2,1)S(1)}, u32[]{:S(2)}, u32[]{:S(2)}) collective-permute-start(bf16[320,1024]{1,0:T(8,128)(2,1)} %get-tuple-element.50), channel_id=1, source_target_pairs={{0,3},{1,0},{2,1},{3,2},{4,7},{5,4},{6,5},{7,6},{8,11},{9,8},{10,9... | collective-permute-start | bytes 1966088 | tf_op jit(solution)/shard_map/ppermute | solution.py:90
  54.9 15.3 %collective-permute-start.10 = (bf16[192,1024]{1,0:T(8,128)(2,1)}, bf16[192,1024]{1,0:T(8,128)(2,1)S(1)}, u32[]{:S(2)}, u32[]{:S(2)}) collective-permute-start(bf16[192,1024]{1,0:T(8,128)(2,1)} %get-tuple-element.54), channel_id=1, source_target_pairs={{0,1},{1,2},{2,3},{3,0},{4,5},{5,6},{6,7},{7,4},{8,9},{9,10},{10,1... | collective-permute-start | bytes 1179656 | tf_op jit(solution)/shard_map/ppermute | solution.py:90
  56.7 19.6 %collective-permute-start.11 = (bf16[192,1024]{1,0:T(8,128)(2,1)}, bf16[192,1024]{1,0:T(8,128)(2,1)S(1)}, u32[]{:S(2)}, u32[]{:S(2)}) collective-permute-start(bf16[192,1024]{1,0:T(8,128)(2,1)} %get-tuple-element.55), channel_id=1, source_target_pairs={{0,2},{1,3},{2,0},{3,1},{4,6},{5,7},{6,4},{7,5},{8,10},{9,11},{10,... | collective-permute-start | bytes 1179656 | tf_op jit(solution)/shard_map/ppermute | solution.py:90
  58.5 23.0 %copy-start.10 = (bf16[320,1024]{1,0:T(8,128)(2,1)}, bf16[320,1024]{1,0:T(8,128)(2,1)S(1)}, u32[]{:S(2)}) copy-start(bf16[320,1024]{1,0:T(8,128)(2,1)S(1)} %collective-permute-done.7.refs_8_) | copy-start | bytes 1966084
  58.5 63.9 %copy-start.1 = (s32[32,8]{0,1:T(8,128)S(1)}, s32[32,8]{0,1:T(8,128)}, u32[]{:S(2)}) copy-start(s32[32,8]{0,1:T(8,128)} %param.13) | copy-start | bytes 3076
  58.5 23.0 %collective-permute-start.12 = (bf16[192,1024]{1,0:T(8,128)(2,1)}, bf16[192,1024]{1,0:T(8,128)(2,1)S(1)}, u32[]{:S(2)}, u32[]{:S(2)}) collective-permute-start(bf16[192,1024]{1,0:T(8,128)(2,1)} %get-tuple-element.56), channel_id=1, source_target_pairs={{0,3},{1,0},{2,1},{3,2},{4,7},{5,4},{6,5},{7,6},{8,11},{9,8},{10,9... | collective-permute-start | bytes 1179656 | tf_op jit(solution)/shard_map/ppermute | solution.py:90
  61.4 20.1 %copy-start.11 = (bf16[320,1024]{1,0:T(8,128)(2,1)}, bf16[320,1024]{1,0:T(8,128)(2,1)S(1)}, u32[]{:S(2)}) copy-start(bf16[320,1024]{1,0:T(8,128)(2,1)S(1)} %collective-permute-done.8.refs_9_) | copy-start | bytes 1966084
  70.2 11.3 %copy-start.12 = (bf16[320,1024]{1,0:T(8,128)(2,1)}, bf16[320,1024]{1,0:T(8,128)(2,1)S(1)}, u32[]{:S(2)}) copy-start(bf16[320,1024]{1,0:T(8,128)(2,1)S(1)} %collective-permute-done.9.refs_10_) | copy-start | bytes 1966084
  70.2 11.3 %copy-start.13 = (bf16[192,1024]{1,0:T(8,128)(2,1)}, bf16[192,1024]{1,0:T(8,128)(2,1)S(1)}, u32[]{:S(2)}) copy-start(bf16[192,1024]{1,0:T(8,128)(2,1)S(1)} %collective-permute-done.10.refs_11_) | copy-start | bytes 1179652
  76.3 5.2 %copy-start.14 = (bf16[192,1024]{1,0:T(8,128)(2,1)}, bf16[192,1024]{1,0:T(8,128)(2,1)S(1)}, u32[]{:S(2)}) copy-start(bf16[192,1024]{1,0:T(8,128)(2,1)S(1)} %collective-permute-done.11.refs_12_) | copy-start | bytes 1179652
  99.7 15.1 %collective-permute-start.13 = (bf16[128,1024]{1,0:T(8,128)(2,1)}, bf16[128,1024]{1,0:T(8,128)(2,1)S(1)}, u32[]{:S(2)}, u32[]{:S(2)}) collective-permute-start(bf16[128,1024]{1,0:T(8,128)(2,1)} %get-tuple-element.66), channel_id=1, source_target_pairs={{0,3},{1,0},{2,1},{3,2},{4,7},{5,4},{6,5},{7,6},{8,11},{9,8},{10,9... | collective-permute-start | bytes 786440 | tf_op jit(solution)/shard_map/ppermute | solution.py:90
  102.3 13.2 %collective-permute-start.14 = (bf16[128,1024]{1,0:T(8,128)(2,1)}, bf16[128,1024]{1,0:T(8,128)(2,1)S(1)}, u32[]{:S(2)}, u32[]{:S(2)}) collective-permute-start(bf16[128,1024]{1,0:T(8,128)(2,1)} %get-tuple-element.67), channel_id=1, source_target_pairs={{0,2},{1,3},{2,0},{3,1},{4,6},{5,7},{6,4},{7,5},{8,10},{9,11},{10,... | collective-permute-start | bytes 786440 | tf_op jit(solution)/shard_map/ppermute | solution.py:90
  103.4 19.0 %collective-permute-start.15 = (bf16[128,1024]{1,0:T(8,128)(2,1)}, bf16[128,1024]{1,0:T(8,128)(2,1)S(1)}, u32[]{:S(2)}, u32[]{:S(2)}) collective-permute-start(bf16[128,1024]{1,0:T(8,128)(2,1)} %get-tuple-element.68), channel_id=1, source_target_pairs={{0,1},{1,2},{2,3},{3,0},{4,5},{5,6},{6,7},{7,4},{8,9},{9,10},{10,1... | collective-permute-start | bytes 786440 | tf_op jit(solution)/shard_map/ppermute | solution.py:90
  104.1 26.3 %collective-permute-start.16 = (bf16[192,1024]{1,0:T(8,128)(2,1)}, bf16[192,1024]{1,0:T(8,128)(2,1)S(1)}, u32[]{:S(2)}, u32[]{:S(2)}) collective-permute-start(bf16[192,1024]{1,0:T(8,128)(2,1)} %get-tuple-element.73), channel_id=1, source_target_pairs={{0,3},{1,0},{2,1},{3,2},{4,7},{5,4},{6,5},{7,6},{8,11},{9,8},{10,9... | collective-permute-start | bytes 1179656 | tf_op jit(solution)/shard_map/ppermute | solution.py:90
  106.6 27.6 %collective-permute-start.17 = (bf16[192,1024]{1,0:T(8,128)(2,1)}, bf16[192,1024]{1,0:T(8,128)(2,1)S(1)}, u32[]{:S(2)}, u32[]{:S(2)}) collective-permute-start(bf16[192,1024]{1,0:T(8,128)(2,1)} %get-tuple-element.74), channel_id=1, source_target_pairs={{0,2},{1,3},{2,0},{3,1},{4,6},{5,7},{6,4},{7,5},{8,10},{9,11},{10,... | collective-permute-start | bytes 1179656 | tf_op jit(solution)/shard_map/ppermute | solution.py:90
  114.8 20.9 %collective-permute-start.18 = (bf16[192,1024]{1,0:T(8,128)(2,1)}, bf16[192,1024]{1,0:T(8,128)(2,1)S(1)}, u32[]{:S(2)}, u32[]{:S(2)}) collective-permute-start(bf16[192,1024]{1,0:T(8,128)(2,1)} %get-tuple-element.75), channel_id=1, source_target_pairs={{0,1},{1,2},{2,3},{3,0},{4,5},{5,6},{6,7},{7,4},{8,9},{9,10},{10,1... | collective-permute-start | bytes 1179656 | tf_op jit(solution)/shard_map/ppermute | solution.py:90
  123.7 6.7 %copy-start.18 = (bf16[128,1024]{1,0:T(8,128)(2,1)S(1)}, bf16[128,1024]{1,0:T(8,128)(2,1)}, u32[]{:S(2)}) copy-start(bf16[128,1024]{1,0:T(8,128)(2,1)} %get-tuple-element.82) | copy-start | bytes 786436
  123.7 10.5 %copy-start.17 = (bf16[128,1024]{1,0:T(8,128)(2,1)S(1)}, bf16[128,1024]{1,0:T(8,128)(2,1)}, u32[]{:S(2)}) copy-start(bf16[128,1024]{1,0:T(8,128)(2,1)} %get-tuple-element.83) | copy-start | bytes 786436
  123.7 12.0 %copy-start.16 = (bf16[128,1024]{1,0:T(8,128)(2,1)S(1)}, bf16[128,1024]{1,0:T(8,128)(2,1)}, u32[]{:S(2)}) copy-start(bf16[128,1024]{1,0:T(8,128)(2,1)} %get-tuple-element.84) | copy-start | bytes 786436
  125.3 10.4 %collective-permute-start.19 = (bf16[128,1024]{1,0:T(8,128)(2,1)S(1)}, bf16[128,1024]{1,0:T(8,128)(2,1)S(1)}, u32[]{:S(2)}, u32[]{:S(2)}) collective-permute-start(bf16[128,1024]{1,0:T(8,128)(2,1)S(1)} %get-tuple-element.76), channel_id=1, source_target_pairs={{0,4},{4,8},{8,12},{12,16},{16,20},{20,24},{24,28},{28,0},{1,5},{5... | collective-permute-start | bytes 786440 | tf_op jit(solution)/shard_map/ppermute | solution.py:90
  125.4 16.9 %copy-start.21 = (bf16[64,1024]{1,0:T(8,128)(2,1)S(1)}, bf16[64,1024]{1,0:T(8,128)(2,1)}, u32[]{:S(2)}) copy-start(bf16[64,1024]{1,0:T(8,128)(2,1)} %get-tuple-element.79) | copy-start | bytes 393220
  125.4 10.3 %collective-permute-start.20 = (bf16[128,1024]{1,0:T(8,128)(2,1)S(1)}, bf16[128,1024]{1,0:T(8,128)(2,1)S(1)}, u32[]{:S(2)}, u32[]{:S(2)}) collective-permute-start(bf16[128,1024]{1,0:T(8,128)(2,1)S(1)} %get-tuple-element.77), channel_id=1, source_target_pairs={{0,28},{4,0},{8,4},{12,8},{16,12},{20,16},{24,20},{28,24},{1,29},{... | collective-permute-start | bytes 786440 | tf_op jit(solution)/shard_map/ppermute | solution.py:90
  130.4 11.8 %collective-permute-start.24 = (bf16[128,1024]{1,0:T(8,128)(2,1)S(1)}, bf16[128,1024]{1,0:T(8,128)(2,1)S(1)}, u32[]{:S(2)}, u32[]{:S(2)}) collective-permute-start(bf16[128,1024]{1,0:T(8,128)(2,1)S(1)} %copy-done.18), channel_id=1, source_target_pairs={{0,3},{1,0},{2,1},{3,2},{4,7},{5,4},{6,5},{7,6},{8,11},{9,8},{10,9... | collective-permute-start | bytes 786440 | tf_op jit(solution)/shard_map/ppermute | solution.py:90
  134.2 10.4 %collective-permute-start.25 = (bf16[128,1024]{1,0:T(8,128)(2,1)S(1)}, bf16[128,1024]{1,0:T(8,128)(2,1)S(1)}, u32[]{:S(2)}, u32[]{:S(2)}) collective-permute-start(bf16[128,1024]{1,0:T(8,128)(2,1)S(1)} %copy-done.17), channel_id=1, source_target_pairs={{0,2},{1,3},{2,0},{3,1},{4,6},{5,7},{6,4},{7,5},{8,10},{9,11},{10,... | collective-permute-start | bytes 786440 | tf_op jit(solution)/shard_map/ppermute | solution.py:90
  135.7 12.1 %collective-permute-start.26 = (bf16[128,1024]{1,0:T(8,128)(2,1)S(1)}, bf16[128,1024]{1,0:T(8,128)(2,1)S(1)}, u32[]{:S(2)}, u32[]{:S(2)}) collective-permute-start(bf16[128,1024]{1,0:T(8,128)(2,1)S(1)} %copy-done.16), channel_id=1, source_target_pairs={{0,1},{1,2},{2,3},{3,0},{4,5},{5,6},{6,7},{7,4},{8,9},{9,10},{10,1... | collective-permute-start | bytes 786440 | tf_op jit(solution)/shard_map/ppermute | solution.py:90
  138.3 9.4 %collective-permute-start.27 = (bf16[128,1024]{1,0:T(8,128)(2,1)S(1)}, bf16[128,1024]{1,0:T(8,128)(2,1)S(1)}, u32[]{:S(2)}, u32[]{:S(2)}) collective-permute-start(bf16[128,1024]{1,0:T(8,128)(2,1)S(1)} %get-tuple-element.85), channel_id=1, source_target_pairs={{0,4},{4,8},{8,12},{12,16},{16,20},{20,24},{24,28},{28,0},{1,5},{5... | collective-permute-start | bytes 786440 | tf_op jit(solution)/shard_map/ppermute | solution.py:90
  138.4 17.8 %collective-permute-start.28 = (bf16[128,1024]{1,0:T(8,128)(2,1)S(1)}, bf16[128,1024]{1,0:T(8,128)(2,1)S(1)}, u32[]{:S(2)}, u32[]{:S(2)}) collective-permute-start(bf16[128,1024]{1,0:T(8,128)(2,1)S(1)} %get-tuple-element.86), channel_id=1, source_target_pairs={{0,28},{4,0},{8,4},{12,8},{16,12},{20,16},{24,20},{28,24},{1,29},{... | collective-permute-start | bytes 786440 | tf_op jit(solution)/shard_map/ppermute | solution.py:90
  142.2 23.6 %collective-permute-start.21 = (bf16[64,1024]{1,0:T(8,128)(2,1)S(1)}, bf16[64,1024]{1,0:T(8,128)(2,1)S(1)}, u32[]{:S(2)}, u32[]{:S(2)}) collective-permute-start(bf16[64,1024]{1,0:T(8,128)(2,1)S(1)} %copy-done.21), channel_id=1, source_target_pairs={{0,3},{1,0},{2,1},{3,2},{4,7},{5,4},{6,5},{7,6},{8,11},{9,8},{10,9... | collective-permute-start | bytes 393224 | tf_op jit(solution)/shard_map/ppermute | solution.py:90
  144.6 18.2 %copy-start.20 = (bf16[64,1024]{1,0:T(8,128)(2,1)S(1)}, bf16[64,1024]{1,0:T(8,128)(2,1)}, u32[]{:S(2)}) copy-start(bf16[64,1024]{1,0:T(8,128)(2,1)} %get-tuple-element.80) | copy-start | bytes 393220
  144.6 21.3 %copy-start.19 = (bf16[64,1024]{1,0:T(8,128)(2,1)S(1)}, bf16[64,1024]{1,0:T(8,128)(2,1)}, u32[]{:S(2)}) copy-start(bf16[64,1024]{1,0:T(8,128)(2,1)} %get-tuple-element.81) | copy-start | bytes 393220
  144.6 27.5 %collective-permute-start.31 = (bf16[128,1024]{1,0:T(8,128)(2,1)S(1)}, bf16[128,1024]{1,0:T(8,128)(2,1)S(1)}, u32[]{:S(2)}, u32[]{:S(2)}) collective-permute-start(bf16[128,1024]{1,0:T(8,128)(2,1)S(1)} %get-tuple-element.89), channel_id=1, source_target_pairs={{0,16},{4,20},{8,24},{12,28},{16,0},{20,4},{24,8},{28,12},{1,17},{... | collective-permute-start | bytes 786440 | tf_op jit(solution)/shard_map/ppermute | solution.py:90
  157.8 14.3 %collective-permute-start.29 = (bf16[128,1024]{1,0:T(8,128)(2,1)S(1)}, bf16[128,1024]{1,0:T(8,128)(2,1)S(1)}, u32[]{:S(2)}, u32[]{:S(2)}) collective-permute-start(bf16[128,1024]{1,0:T(8,128)(2,1)S(1)} %get-tuple-element.87), channel_id=1, source_target_pairs={{0,4},{4,8},{8,12},{12,16},{16,20},{20,24},{24,28},{28,0},{1,5},{5... | collective-permute-start | bytes 786440 | tf_op jit(solution)/shard_map/ppermute | solution.py:90
  157.9 14.2 %collective-permute-start.30 = (bf16[128,1024]{1,0:T(8,128)(2,1)S(1)}, bf16[128,1024]{1,0:T(8,128)(2,1)S(1)}, u32[]{:S(2)}, u32[]{:S(2)}) collective-permute-start(bf16[128,1024]{1,0:T(8,128)(2,1)S(1)} %get-tuple-element.88), channel_id=1, source_target_pairs={{0,28},{4,0},{8,4},{12,8},{16,12},{20,16},{24,20},{28,24},{1,29},{... | collective-permute-start | bytes 786440 | tf_op jit(solution)/shard_map/ppermute | solution.py:90
  162.8 7.7 %collective-permute-start.22 = (bf16[64,1024]{1,0:T(8,128)(2,1)S(1)}, bf16[64,1024]{1,0:T(8,128)(2,1)S(1)}, u32[]{:S(2)}, u32[]{:S(2)}) collective-permute-start(bf16[64,1024]{1,0:T(8,128)(2,1)S(1)} %copy-done.20), channel_id=1, source_target_pairs={{0,2},{1,3},{2,0},{3,1},{4,6},{5,7},{6,4},{7,5},{8,10},{9,11},{10,... | collective-permute-start | bytes 393224 | tf_op jit(solution)/shard_map/ppermute | solution.py:90
  165.9 6.2 %collective-permute-start.23 = (bf16[64,1024]{1,0:T(8,128)(2,1)S(1)}, bf16[64,1024]{1,0:T(8,128)(2,1)S(1)}, u32[]{:S(2)}, u32[]{:S(2)}) collective-permute-start(bf16[64,1024]{1,0:T(8,128)(2,1)S(1)} %copy-done.19), channel_id=1, source_target_pairs={{0,1},{1,2},{2,3},{3,0},{4,5},{5,6},{6,7},{7,4},{8,9},{9,10},{10,1... | collective-permute-start | bytes 393224 | tf_op jit(solution)/shard_map/ppermute | solution.py:90
  (6 other events, 6.1 us)
where the time goes:
time: 175 us; the launch traced here: 174 us
  waiting for transfers between devices  74.5 us (43%)
  starting transfers between devices  61.9 us (35%)
  Pallas kernels  33.1 us (19%)
  local copies, waits for them, and re-layouts  3.61 us (2%)
    ppermute x32, waiting for transfers between devices, shift(): lax.ppermute(array, axis, [(i, (i + by) % size) for i in range(size)])  74.5 us
    ppermute x32, starting transfers between devices, shift(): lax.ppermute(array, axis, [(i, (i + by) % size) for i in range(size)])  61.9 us
    pallas_call x1, Pallas kernels, attend(): pl.pallas_call(attend_body, grid=(KV_HEADS,), out_shape=outs, in_specs=[S...  17.4 us
    pallas_call x4, Pallas kernels, combine(): pl.pallas_call(body, out_shape=shapes, in_specs=[SM, FAR] + [ANY] * (3 +...  7.72 us
    pallas_call x2, Pallas kernels, pack(): pl.pallas_call(body, out_shape=[like(count * BLK)] * 3, in_specs=[SM] + [...  6.32 us
    unnamed x44, local copies, waits for them, and re-layouts  3.61 us
  transfers between devices with their start and end apart: 32, of which 17 were waited for; matrix products, arithmetic and copies ran while one was open for 0% of the time, Pallas kernels for 5%

commit v1 on v0

--- a/solution.py
+++ b/solution.py
@@ -25,13 +25,12 @@
 LOG2E = math.log2(math.e)
 HIDDEN = -1e30
 
-FETCH = ((0, 1, -1, 2, -2), (3, -3, 4))
+FETCH = ((0,), (1, -1, 2, -2), (3, -3, 4))
 GIVE = ((3, -3), (2, -2, 4), (1, -1), (0,))
 COLUMN = (0, 1, -1, 2, -2, 3, -3, 4)
 
 VM = pl.BlockSpec(memory_space=pltpu.VMEM)
 ANY = pl.BlockSpec(memory_space=pl.ANY)
-FAR = pl.BlockSpec(memory_space=pltpu.HBM)
 SM = pl.BlockSpec(memory_space=pltpu.SMEM)
 
 
@@ -94,34 +93,44 @@
     return [shift(a, "y", YN, sign * m) for m, a in zip((1, 2, 3), arrays)]
 
 
-def join(key_states, value_states):
-    def body(k, v, kv):
+def join(needed, key_states, value_states):
+    def body(needed, k, v, kv, *outs):
         kv[:, :KVW] = k[...]
         kv[:, KVW:] = v[...]
 
-    return pl.pallas_call(
+        def copy(m, i, part):
+            outs[m - 1][:, :KVW] = half(k, part)[...]
+            outs[m - 1][:, KVW:] = half(v, part)[...]
+
+        each_listed(needed, (0,), copy)
+
+    got = pl.pallas_call(
         body,
-        out_shape=like(TOK),
-        in_specs=[VM, VM],
-        out_specs=VM,
+        out_shape=[like(TOK)] + [like(BLK)] * 3,
+        in_specs=[SM, VM, VM],
+        out_specs=[VM] * 4,
         name="join",
-    )(key_states, value_states)
-
-
-def gather(kv, needed):
+    )(needed, key_states, value_states)
+    return got[0], got[1:]
+
+
+def gather(kv, mine, needed):
     shards = {0: kv}
     shards[1], shards[-1] = shift(kv, "z", ZN, -1), shift(kv, "z", ZN, 1)
     shards[2], shards[-2] = shift(shards[1], "z", ZN, -1), shift(shards[-1], "z", ZN, 1)
+    zeroth = to_mates(mine, 1)
 
     def packed(b):
         return pack(needed, [shards[k] for k in FETCH[b]], FETCH[b])
 
-    mine = packed(0)
+    shards[2], zeroth = lax.optimization_barrier((shards[2], zeroth))
+    mine = packed(1)
     first = to_mates(mine, 1)
-    up, down, far, mine = lax.optimization_barrier((shards[2], shards[-2], kv, mine))
+    up, down, mine = lax.optimization_barrier((shards[2], shards[-2], mine))
     shards[3], shards[-3] = shift(up, "z", ZN, -1), shift(down, "z", ZN, 1)
+    far, shards[3] = lax.optimization_barrier((kv, shards[3]))
     shards[4] = shift(far, "z", ZN, 4)
-    return shards, [first, to_mates(packed(1), 1)]
+    return shards, [zeroth, first, to_mates(packed(2), 1)]
 
 
 def attend_body(needed, plan, lengths, q_ref, do_ref, *refs):
@@ -246,21 +255,20 @@
 
     @pl.when(g == KV_HEADS - 1)
     def _():
-        whole = pltpu.make_async_copy(grad, grad_out, sems.at[NEED])
+        whole = pltpu.make_async_copy(
+            grad.at[pl.ds(0, TOK), :], grad_out.at[pl.ds(0, TOK), :], sems.at[NEED]
+        )
         whole.start()
 
-        def send(j, b, i, m, k):
+        def give(j, b, i, m, k):
             if m > 0:
                 target = mate_out[b][m - 1].at[pl.ds(i * BLK, BLK), :]
-                pltpu.make_async_copy(grad.at[slot_rows(j), :], target, sems.at[j]).start()
-
-        def sent(j, b, i, m, k):
-            if m > 0:
-                target = mate_out[b][m - 1].at[pl.ds(i * BLK, BLK), :]
-                pltpu.make_async_copy(grad.at[slot_rows(j), :], target, sems.at[j]).wait()
-
-        each_source(GIVE, send)
-        each_source(GIVE, sent)
+            else:
+                target = grad_out.at[slot_rows(j), :]
+            return pltpu.make_async_copy(grad.at[slot_rows(j), :], target, sems.at[j])
+
+        each_source(GIVE, lambda *at: give(*at).start())
+        each_source(GIVE, lambda *at: give(*at).wait())
         whole.wait()
 
 
@@ -366,7 +374,7 @@
     return pl.pallas_call(
         body,
         out_shape=shapes,
-        in_specs=[SM, FAR] + [ANY] * (3 + len(extra)),
+        in_specs=[SM] + [ANY] * (4 + len(extra)),
         out_specs=[VM] * len(shapes),
         scratch_shapes=[
             pltpu.VMEM((n, TOK, 2 * KVW), jnp.float32),
@@ -401,7 +409,8 @@
 
 def on_device(queries, key_states, value_states, grads_out, lengths, plan, needed):
     needed = needed.T
-    shards, received = gather(join(key_states, value_states), needed)
+    kv, mine = join(needed, key_states, value_states)
+    shards, received = gather(kv, mine, needed)
     outputs, query_grads, grad, mates = attend(
         queries, grads_out, lengths, plan, needed, shards, received
     )

time: 175 us -> 173 us (0.989)
  waiting for transfers between devices: 74.5 us -> 64.1 us
  starting transfers between devices: 61.9 us -> 71.4 us
  Pallas kernels: 33.1 us -> 31.1 us
    ppermute x32 -> x35, waiting for transfers between devices: 74.5 us -> 64.1 us  [shift(): lax.ppermute(array, axis, [(i, (i + by) % size) for i in range(size)])]
    ppermute x32 -> x35, starting transfers between devices: 61.9 us -> 71.4 us  [shift(): lax.ppermute(array, axis, [(i, (i + by) % size) for i in range(size)])]
    pallas_call x2, Pallas kernels: 6.32 us -> 4.53 us  [pack(): pl.pallas_call(body, out_shape=[like(count * BLK)] * 3, in_specs=[SM] + [...]
    unnamed x44 -> x48, local copies, waits for them, and re-layouts: 3.61 us -> 5 us
  transfers between devices with their start and end apart: 32 -> 35, of which waited for: 17 -> 15; matrix products, arithmetic and copies ran while one was open for 0% -> 0% of each run, Pallas kernels for 5% -> 5%
where the time goes in v1:
time: 173 us
  starting transfers between devices  71.4 us (41%)
  waiting for transfers between devices  64.1 us (37%)
  Pallas kernels  31.1 us (18%)
  local copies, waits for them, and re-layouts  5 us (3%)
    ppermute x35, starting transfers between devices, shift(): lax.ppermute(array, axis, [(i, (i + by) % size) for i in range(size)])  71.4 us
    ppermute x35, waiting for transfers between devices, shift(): lax.ppermute(array, axis, [(i, (i + by) % size) for i in range(size)])  64.1 us
    pallas_call x1, Pallas kernels, attend(): pl.pallas_call(attend_body, grid=(KV_HEADS,), out_shape=outs, in_specs=[S...  17 us
    pallas_call x4, Pallas kernels, combine(): pl.pallas_call(body, out_shape=shapes, in_specs=[SM] + [ANY] * (4 + len(e...  7.65 us
    unnamed x48, local copies, waits for them, and re-layouts  5 us
    pallas_call x2, Pallas kernels, pack(): pl.pallas_call(body, out_shape=[like(count * BLK)] * 3, in_specs=[SM] + [...  4.53 us
  transfers between devices with their start and end apart: 35, of which 15 were waited for; matrix products, arithmetic and copies ran while one was open for 0% of the time, Pallas kernels for 5%

profile of v1, /device:TPU:4, one launch (start us, length us, event | category | flops | bytes accessed | tf_op | source)
XLA Modules:
  0.0 172.6 jit_solution(7267196794684704396)
XLA Ops:
  0.6 1.9 %join.1 = (bf16[128,1024]{1,0:T(8,128)(2,1)}, bf16[64,1024]{1,0:T(8,128)(2,1)}, bf16[64,1024]{1,0:T(8,128)(2,1)}, bf16[64,1024]{1,0:T(8,128)(2,1)}) custom-call(s32[8,32]{1,0:T(8,128)} %bitcast.1, bf16[128,512]{1,0:T(8,128)(2,1)} %k.1, bf16[128,512]{1,0:T(8,128)(2,1)} %v.1), custom_call_target="tpu_custom_call" | custom-call | tf_op jit(solution)/shard_map/join/pallas_call | solution.py:107
  2.5 5.9 %collective-permute-start = (bf16[128,1024]{1,0:T(8,128)(2,1)}, bf16[128,1024]{1,0:T(8,128)(2,1)S(1)}, u32[]{:S(2)}, u32[]{:S(2)}) collective-permute-start(bf16[128,1024]{1,0:T(8,128)(2,1)} %get-tuple-element.68.refs_0_), channel_id=1, source_target_pairs={{0,28},{4,0},{8,4},{12,8},{16,12},{20,16},{24,20},{28,24},{1,29},{... | collective-permute-start | bytes 786440 | tf_op jit(solution)/shard_map/ppermute | solution.py:89
  8.4 5.9 %collective-permute-done.refs_0_.refs_1_ = bf16[128,1024]{1,0:T(8,128)(2,1)S(1)} collective-permute-done((bf16[128,1024]{1,0:T(8,128)(2,1)}, bf16[128,1024]{1,0:T(8,128)(2,1)S(1)}, u32[]{:S(2)}, u32[]{:S(2)}) %collective-permute-start) | collective-permute-done | bytes 262176 | tf_op jit(solution)/shard_map/ppermute | solution.py:89
  14.3 3.6 %collective-permute-start.2 = (bf16[128,1024]{1,0:T(8,128)(2,1)S(1)}, bf16[128,1024]{1,0:T(8,128)(2,1)S(1)}, u32[]{:S(2)}, u32[]{:S(2)}) collective-permute-start(bf16[128,1024]{1,0:T(8,128)(2,1)S(1)} %collective-permute-done.refs_0_.refs_1_), channel_id=1, source_target_pairs={{0,28},{4,0},{8,4},{12,8},{16,12},{20,16},{24,20},{28,24},{1,29},{... | collective-permute-start | bytes 786440 | tf_op jit(solution)/shard_map/ppermute | solution.py:89
  17.9 1.7 collective-permute-start.3
  19.5 2.9 %collective-permute-start.4 = (bf16[64,1024]{1,0:T(8,128)(2,1)}, bf16[64,1024]{1,0:T(8,128)(2,1)S(1)}, u32[]{:S(2)}, u32[]{:S(2)}) collective-permute-start(bf16[64,1024]{1,0:T(8,128)(2,1)} %get-tuple-element.59), channel_id=1, source_target_pairs={{0,2},{1,3},{2,0},{3,1},{4,6},{5,7},{6,4},{7,5},{8,10},{9,11},{10,... | collective-permute-start | bytes 393224 | tf_op jit(solution)/shard_map/ppermute | solution.py:89
  22.4 1.3 collective-permute-start.5
  23.8 2.0 %collective-permute-done.3.refs_8_ = bf16[64,1024]{1,0:T(8,128)(2,1)S(1)} collective-permute-done((bf16[64,1024]{1,0:T(8,128)(2,1)}, bf16[64,1024]{1,0:T(8,128)(2,1)S(1)}, u32[]{:S(2)}, u32[]{:S(2)}) %collective-permute-start.3) | collective-permute-done | bytes 131104 | tf_op jit(solution)/shard_map/ppermute | solution.py:89
  25.7 1.8 %collective-permute-done.4.refs_9_ = bf16[64,1024]{1,0:T(8,128)(2,1)S(1)} collective-permute-done((bf16[64,1024]{1,0:T(8,128)(2,1)}, bf16[64,1024]{1,0:T(8,128)(2,1)S(1)}, u32[]{:S(2)}, u32[]{:S(2)}) %collective-permute-start.4) | collective-permute-done | bytes 131104 | tf_op jit(solution)/shard_map/ppermute | solution.py:89
  29.1 2.4 %pack.2 = (bf16[256,1024]{1,0:T(8,128)(2,1)}, bf16[256,1024]{1,0:T(8,128)(2,1)}, bf16[256,1024]{1,0:T(8,128)(2,1)}) custom-call(s32[8,32]{1,0:T(8,128)} %bitcast.2, bf16[128,1024]{1,0:T(8,128)(2,1)} %copy-done.5, bf16[128,1024]{1,0:T(8,128)(2,1)} %copy-done.6, bf16[128,1024]{1,0:T(8,128)(2,1)} %copy-done.7, bf16[128,1024]{1,0:T(8,128)(2,1)} %copy-done.8), custom_call_target="tpu_custom_call" | custom-call | tf_op jit(solution)/shard_map/pack/pallas_call | solution.py:78
  31.5 4.0 %collective-permute-start.7 = (bf16[128,1024]{1,0:T(8,128)(2,1)}, bf16[128,1024]{1,0:T(8,128)(2,1)S(1)}, u32[]{:S(2)}, u32[]{:S(2)}) collective-permute-start(bf16[128,1024]{1,0:T(8,128)(2,1)} %copy-done.7), channel_id=1, source_target_pairs={{0,28},{4,0},{8,4},{12,8},{16,12},{20,16},{24,20},{28,24},{1,29},{... | collective-permute-start | bytes 786440 | tf_op jit(solution)/shard_map/ppermute | solution.py:89
  35.5 1.0 collective-permute-start.10
  36.5 6.1 %collective-permute-done.7.refs_0_.refs_5_ = bf16[128,1024]{1,0:T(8,128)(2,1)S(1)} collective-permute-done((bf16[128,1024]{1,0:T(8,128)(2,1)}, bf16[128,1024]{1,0:T(8,128)(2,1)S(1)}, u32[]{:S(2)}, u32[]{:S(2)}) %collective-permute-start.7) | collective-permute-done | bytes 262176 | tf_op jit(solution)/shard_map/ppermute | solution.py:89
  42.6 2.1 %collective-permute-start.11 = (bf16[256,1024]{1,0:T(8,128)(2,1)}, bf16[256,1024]{1,0:T(8,128)(2,1)S(1)}, u32[]{:S(2)}, u32[]{:S(2)}) collective-permute-start(bf16[256,1024]{1,0:T(8,128)(2,1)} %get-tuple-element.63), channel_id=1, source_target_pairs={{0,2},{1,3},{2,0},{3,1},{4,6},{5,7},{6,4},{7,5},{8,10},{9,11},{10,... | collective-permute-start | bytes 1572872 | tf_op jit(solution)/shard_map/ppermute | solution.py:89
  44.6 1.6 collective-permute-start.12
  46.2 9.3 %collective-permute-done.8.refs_1_.refs_6_ = bf16[128,1024]{1,0:T(8,128)(2,1)S(1)} collective-permute-done((bf16[128,1024]{1,0:T(8,128)(2,1)}, bf16[128,1024]{1,0:T(8,128)(2,1)S(1)}, u32[]{:S(2)}, u32[]{:S(2)}) %collective-permute-start.8) | collective-permute-done | bytes 262176 | tf_op jit(solution)/shard_map/ppermute | solution.py:89
  57.0 2.2 %pack.3 = (bf16[192,1024]{1,0:T(8,128)(2,1)}, bf16[192,1024]{1,0:T(8,128)(2,1)}, bf16[192,1024]{1,0:T(8,128)(2,1)}) custom-call(s32[8,32]{1,0:T(8,128)} %bitcast.3, bf16[128,1024]{1,0:T(8,128)(2,1)} %copy-done.2, bf16[128,1024]{1,0:T(8,128)(2,1)} %copy-done.3, bf16[128,1024]{1,0:T(8,128)(2,1)} %copy-done.4), custom_call_target="tpu_custom_call" | custom-call | tf_op jit(solution)/shard_map/pack/pallas_call | solution.py:78
  59.7 3.2 %collective-permute-start.14 = (bf16[192,1024]{1,0:T(8,128)(2,1)}, bf16[192,1024]{1,0:T(8,128)(2,1)S(1)}, u32[]{:S(2)}, u32[]{:S(2)}) collective-permute-start(bf16[192,1024]{1,0:T(8,128)(2,1)} %get-tuple-element.73), channel_id=1, source_target_pairs={{0,2},{1,3},{2,0},{3,1},{4,6},{5,7},{6,4},{7,5},{8,10},{9,11},{10,... | collective-permute-start | bytes 1179656 | tf_op jit(solution)/shard_map/ppermute | solution.py:89
  62.9 1.9 %collective-permute-start.15 = (bf16[192,1024]{1,0:T(8,128)(2,1)}, bf16[192,1024]{1,0:T(8,128)(2,1)S(1)}, u32[]{:S(2)}, u32[]{:S(2)}) collective-permute-start(bf16[192,1024]{1,0:T(8,128)(2,1)} %get-tuple-element.74), channel_id=1, source_target_pairs={{0,3},{1,0},{2,1},{3,2},{4,7},{5,4},{6,5},{7,6},{8,11},{9,8},{10,9... | collective-permute-start | bytes 1179656 | tf_op jit(solution)/shard_map/ppermute | solution.py:89
  64.9 5.2 %collective-permute-done.12.refs_13_ = bf16[256,1024]{1,0:T(8,128)(2,1)S(1)} collective-permute-done((bf16[256,1024]{1,0:T(8,128)(2,1)}, bf16[256,1024]{1,0:T(8,128)(2,1)S(1)}, u32[]{:S(2)}, u32[]{:S(2)}) %collective-permute-start.12) | collective-permute-done | bytes 524320 | tf_op jit(solution)/shard_map/ppermute | solution.py:89
  70.1 7.7 %collective-permute-done.13.refs_14_ = bf16[192,1024]{1,0:T(8,128)(2,1)S(1)} collective-permute-done((bf16[192,1024]{1,0:T(8,128)(2,1)}, bf16[192,1024]{1,0:T(8,128)(2,1)S(1)}, u32[]{:S(2)}, u32[]{:S(2)}) %collective-permute-start.13) | collective-permute-done | bytes 393248 | tf_op jit(solution)/shard_map/ppermute | solution.py:89
  77.7 4.1 %collective-permute-done.15.refs_16_ = bf16[192,1024]{1,0:T(8,128)(2,1)S(1)} collective-permute-done((bf16[192,1024]{1,0:T(8,128)(2,1)}, bf16[192,1024]{1,0:T(8,128)(2,1)S(1)}, u32[]{:S(2)}, u32[]{:S(2)}) %collective-permute-start.15) | collective-permute-done | bytes 393248 | tf_op jit(solution)/shard_map/ppermute | solution.py:89
  82.6 17.0 %attend.1 = (bf16[128,4096]{1,0:T(8,128)(2,1)}, bf16[128,4096]{1,0:T(8,128)(2,1)}, bf16[640,1024]{1,0:T(8,128)(2,1)}, bf16[128,1024]{1,0:T(8,128)(2,1)}, bf16[12...) custom-call(s32[8,32]{1,0:T(8,128)} %bitcast.4, ...), custom_call_target="tpu_custom_call" | custom-call | tf_op jit(solution)/shard_map/attend/pallas_call | solution.py:284
  99.6 2.5 %collective-permute-start.16 = (bf16[128,1024]{1,0:T(8,128)(2,1)}, bf16[128,1024]{1,0:T(8,128)(2,1)S(1)}, u32[]{:S(2)}, u32[]{:S(2)}) collective-permute-start(bf16[128,1024]{1,0:T(8,128)(2,1)} %get-tuple-element.84), channel_id=1, source_target_pairs={{0,3},{1,0},{2,1},{3,2},{4,7},{5,4},{6,5},{7,6},{8,11},{9,8},{10,9... | collective-permute-start | bytes 786440 | tf_op jit(solution)/shard_map/ppermute | solution.py:89
  102.1 0.9 collective-permute-start.18
  103.1 2.3 %collective-permute-start.19 = (bf16[192,1024]{1,0:T(8,128)(2,1)}, bf16[192,1024]{1,0:T(8,128)(2,1)S(1)}, u32[]{:S(2)}, u32[]{:S(2)}) collective-permute-start(bf16[192,1024]{1,0:T(8,128)(2,1)} %get-tuple-element.91), channel_id=1, source_target_pairs={{0,3},{1,0},{2,1},{3,2},{4,7},{5,4},{6,5},{7,6},{8,11},{9,8},{10,9... | collective-permute-start | bytes 1179656 | tf_op jit(solution)/shard_map/ppermute | solution.py:89
  105.4 2.3 %collective-permute-start.20 = (bf16[192,1024]{1,0:T(8,128)(2,1)}, bf16[192,1024]{1,0:T(8,128)(2,1)S(1)}, u32[]{:S(2)}, u32[]{:S(2)}) collective-permute-start(bf16[192,1024]{1,0:T(8,128)(2,1)} %get-tuple-element.92), channel_id=1, source_target_pairs={{0,2},{1,3},{2,0},{3,1},{4,6},{5,7},{6,4},{7,5},{8,10},{9,11},{10,... | collective-permute-start | bytes 1179656 | tf_op jit(solution)/shard_map/ppermute | solution.py:89
  107.7 6.9 %collective-permute-done.16.refs_0_ = bf16[128,1024]{1,0:T(8,128)(2,1)S(1)} collective-permute-done((bf16[128,1024]{1,0:T(8,128)(2,1)}, bf16[128,1024]{1,0:T(8,128)(2,1)S(1)}, u32[]{:S(2)}, u32[]{:S(2)}) %collective-permute-start.16) | collective-permute-done | bytes 262176 | tf_op jit(solution)/shard_map/ppermute | solution.py:89
  114.5 4.2 %collective-permute-done.18.refs_2_ = bf16[128,1024]{1,0:T(8,128)(2,1)S(1)} collective-permute-done((bf16[128,1024]{1,0:T(8,128)(2,1)}, bf16[128,1024]{1,0:T(8,128)(2,1)S(1)}, u32[]{:S(2)}, u32[]{:S(2)}) %collective-permute-start.18) | collective-permute-done | bytes 262176 | tf_op jit(solution)/shard_map/ppermute | solution.py:89
  118.8 1.3 copy-done
  120.1 1.8 %combine.4 = (bf16[128,1024]{1,0:T(8,128)(2,1)S(1)}, bf16[128,1024]{1,0:T(8,128)(2,1)S(1)}) custom-call(s32[8,32]{1,0:T(8,128)S(1)} %bitcast.5, bf16[640,1024]{1,0:T(8,128)(2,1)S(1)} %copy-done, bf16[128,1024]{1,0:T(8,128)(2,1)S(1)} %collective-permute-done.16.refs_0_, bf16[128,1024]{1,0:T(8,128)(2,1)S(1)} %collective-permute-done.17.refs_1_, ...), custom_call_target="tpu_custom_call" | custom-call | tf_op jit(solution)/shard_map/combine/pallas_call | solution.py:374
  122.2 7.2 %collective-permute-start.23 = (bf16[128,1024]{1,0:T(8,128)(2,1)S(1)}, bf16[128,1024]{1,0:T(8,128)(2,1)S(1)}, u32[]{:S(2)}, u32[]{:S(2)}) collective-permute-start(bf16[128,1024]{1,0:T(8,128)(2,1)S(1)} %get-tuple-element.95), channel_id=1, source_target_pairs={{0,28},{4,0},{8,4},{12,8},{16,12},{20,16},{24,20},{28,24},{1,29},{... | collective-permute-start | bytes 786440 | tf_op jit(solution)/shard_map/ppermute | solution.py:89
  129.4 1.1 collective-permute-done.19.refs_0_
  130.5 3.6 %collective-permute-start.27 = (bf16[128,1024]{1,0:T(8,128)(2,1)S(1)}, bf16[128,1024]{1,0:T(8,128)(2,1)S(1)}, u32[]{:S(2)}, u32[]{:S(2)}) collective-permute-start(bf16[128,1024]{1,0:T(8,128)(2,1)S(1)} %copy-done.20), channel_id=1, source_target_pairs={{0,3},{1,0},{2,1},{3,2},{4,7},{5,4},{6,5},{7,6},{8,11},{9,8},{10,9... | collective-permute-start | bytes 786440 | tf_op jit(solution)/shard_map/ppermute | solution.py:89
  134.1 1.2 collective-permute-start.29
  135.3 2.3 %combine.5 = (bf16[128,1024]{1,0:T(8,128)(2,1)S(1)}, bf16[128,1024]{1,0:T(8,128)(2,1)S(1)}, bf16[128,1024]{1,0:T(8,128)(2,1)S(1)}) custom-call(s32[8,32]{1,0:T(8,128)S(1)} %bitcast.6, bf16[640,1024]{1,0:T(8,128)(2,1)S(1)} %copy-done, bf16[192,1024]{1,0:T(8,128)(2,1)S(1)} %collective-permute-done.19.refs_0_, ...), custom_call_target="tpu_custom_call" | custom-call | tf_op jit(solution)/shard_map/combine/pallas_call | solution.py:374
  137.6 0.9 collective-permute-start.30
  138.5 2.4 %collective-permute-start.31 = (bf16[128,1024]{1,0:T(8,128)(2,1)S(1)}, bf16[128,1024]{1,0:T(8,128)(2,1)S(1)}, u32[]{:S(2)}, u32[]{:S(2)}) collective-permute-start(bf16[128,1024]{1,0:T(8,128)(2,1)S(1)} %get-tuple-element.104), channel_id=1, source_target_pairs={{0,28},{4,0},{8,4},{12,8},{16,12},{20,16},{24,20},{28,24},{1,29},{... | collective-permute-start | bytes 786440 | tf_op jit(solution)/shard_map/ppermute | solution.py:89
  140.9 3.6 %collective-permute-done.27.refs_0_ = bf16[128,1024]{1,0:T(8,128)(2,1)S(1)} collective-permute-done((bf16[128,1024]{1,0:T(8,128)(2,1)S(1)}, bf16[128,1024]{1,0:T(8,128)(2,1)S(1)}, u32[]{:S(2)}, u32[]{:S(2)}) %collective-permute-start.27) | collective-permute-done | bytes 262176 | tf_op jit(solution)/shard_map/ppermute | solution.py:89
  144.5 3.7 %collective-permute-start.24 = (bf16[64,1024]{1,0:T(8,128)(2,1)S(1)}, bf16[64,1024]{1,0:T(8,128)(2,1)S(1)}, u32[]{:S(2)}, u32[]{:S(2)}) collective-permute-start(bf16[64,1024]{1,0:T(8,128)(2,1)S(1)} %copy-done.23), channel_id=1, source_target_pairs={{0,3},{1,0},{2,1},{3,2},{4,7},{5,4},{6,5},{7,6},{8,11},{9,8},{10,9... | collective-permute-start | bytes 393224 | tf_op jit(solution)/shard_map/ppermute | solution.py:89
  148.2 1.7 collective-permute-start.34
  149.9 1.8 %combine.6 = (bf16[128,1024]{1,0:T(8,128)(2,1)S(1)}, bf16[128,1024]{1,0:T(8,128)(2,1)S(1)}) custom-call(s32[8,32]{1,0:T(8,128)S(1)} %bitcast.7, bf16[640,1024]{1,0:T(8,128)(2,1)S(1)} %copy-done, bf16[128,1024]{1,0:T(8,128)(2,1)S(1)} %collective-permute-done.27.refs_0_, bf16[128,1024]{1,0:T(8,128)(2,1)S(1)} %collective-permute-done.28.refs_1_, ...), custom_call_target="tpu_custom_call" | custom-call | tf_op jit(solution)/shard_map/combine/pallas_call | solution.py:374
  151.8 2.2 %collective-permute-start.32 = (bf16[128,1024]{1,0:T(8,128)(2,1)S(1)}, bf16[128,1024]{1,0:T(8,128)(2,1)S(1)}, u32[]{:S(2)}, u32[]{:S(2)}) collective-permute-start(bf16[128,1024]{1,0:T(8,128)(2,1)S(1)} %get-tuple-element.105), channel_id=1, source_target_pairs={{0,4},{4,8},{8,12},{12,16},{16,20},{20,24},{24,28},{28,0},{1,5},{5... | collective-permute-start | bytes 786440 | tf_op jit(solution)/shard_map/ppermute | solution.py:89
  153.9 1.1 collective-permute-start.33
  155.1 9.4 %collective-permute-start.25 = (bf16[64,1024]{1,0:T(8,128)(2,1)S(1)}, bf16[64,1024]{1,0:T(8,128)(2,1)S(1)}, u32[]{:S(2)}, u32[]{:S(2)}) collective-permute-start(bf16[64,1024]{1,0:T(8,128)(2,1)S(1)} %copy-done.22), channel_id=1, source_target_pairs={{0,2},{1,3},{2,0},{3,1},{4,6},{5,7},{6,4},{7,5},{8,10},{9,11},{10,... | collective-permute-start | bytes 393224 | tf_op jit(solution)/shard_map/ppermute | solution.py:89
  164.5 2.9 %collective-permute-done.25.refs_1_ = bf16[64,1024]{1,0:T(8,128)(2,1)S(1)} collective-permute-done((bf16[64,1024]{1,0:T(8,128)(2,1)S(1)}, bf16[64,1024]{1,0:T(8,128)(2,1)S(1)}, u32[]{:S(2)}, u32[]{:S(2)}) %collective-permute-start.25) | collective-permute-done | bytes 131104 | tf_op jit(solution)/shard_map/ppermute | solution.py:89
  167.4 3.2 %collective-permute-done.26.refs_2_ = bf16[64,1024]{1,0:T(8,128)(2,1)S(1)} collective-permute-done((bf16[64,1024]{1,0:T(8,128)(2,1)S(1)}, bf16[64,1024]{1,0:T(8,128)(2,1)S(1)}, u32[]{:S(2)}, u32[]{:S(2)}) %collective-permute-start.26) | collective-permute-done | bytes 131104 | tf_op jit(solution)/shard_map/ppermute | solution.py:89
  170.7 1.8 %combine.7 = (bf16[128,512]{1,0:T(8,128)(2,1)}, bf16[128,512]{1,0:T(8,128)(2,1)}) custom-call(s32[8,32]{1,0:T(8,128)S(1)} %bitcast.8, bf16[640,1024]{1,0:T(8,128)(2,1)S(1)} %copy-done, bf16[64,1024]{1,0:T(8,128)(2,1)S(1)} %collective-permute-done.24.refs_0_, bf16[64,1024]{1,0:T(8,128)(2,1)S(1)} %collective-permute-done.25.refs_1_, ...), custom_call_target="tpu_custom_call" | custom-call | tf_op jit(solution)/shard_map/combine/pallas_call | solution.py:374
  (78 shorter events, 4.8 us)
Async XLA Ops:
  2.5 11.7 %collective-permute-start = (bf16[128,1024]{1,0:T(8,128)(2,1)}, bf16[128,1024]{1,0:T(8,128)(2,1)S(1)}, u32[]{:S(2)}, u32[]{:S(2)}) collective-permute-start(bf16[128,1024]{1,0:T(8,128)(2,1)} %get-tuple-element.68.refs_0_), channel_id=1, source_target_pairs={{0,28},{4,0},{8,4},{12,8},{16,12},{20,16},{24,20},{28,24},{1,29},{... | collective-permute-start | bytes 786440 | tf_op jit(solution)/shard_map/ppermute | solution.py:89
  8.4 9.5 %collective-permute-start.1 = (bf16[128,1024]{1,0:T(8,128)(2,1)}, bf16[128,1024]{1,0:T(8,128)(2,1)S(1)}, u32[]{:S(2)}, u32[]{:S(2)}) collective-permute-start(bf16[128,1024]{1,0:T(8,128)(2,1)} %get-tuple-element.68.refs_0_), channel_id=1, source_target_pairs={{0,4},{4,8},{8,12},{12,16},{16,20},{20,24},{24,28},{28,0},{1,5},{5... | collective-permute-start | bytes 786440 | tf_op jit(solution)/shard_map/ppermute | solution.py:89
  14.3 13.3 %copy-start.5 = (bf16[128,1024]{1,0:T(8,128)(2,1)}, bf16[128,1024]{1,0:T(8,128)(2,1)S(1)}, u32[]{:S(2)}) copy-start(bf16[128,1024]{1,0:T(8,128)(2,1)S(1)} %collective-permute-done.refs_0_.refs_1_) | copy-start | bytes 786436
  14.3 13.3 %collective-permute-start.2 = (bf16[128,1024]{1,0:T(8,128)(2,1)S(1)}, bf16[128,1024]{1,0:T(8,128)(2,1)S(1)}, u32[]{:S(2)}, u32[]{:S(2)}) collective-permute-start(bf16[128,1024]{1,0:T(8,128)(2,1)S(1)} %collective-permute-done.refs_0_.refs_1_), channel_id=1, source_target_pairs={{0,28},{4,0},{8,4},{12,8},{16,12},{20,16},{24,20},{28,24},{1,29},{... | collective-permute-start | bytes 786440 | tf_op jit(solution)/shard_map/ppermute | solution.py:89
  17.9 9.8 %collective-permute-start.6 = (bf16[128,1024]{1,0:T(8,128)(2,1)S(1)}, bf16[128,1024]{1,0:T(8,128)(2,1)S(1)}, u32[]{:S(2)}, u32[]{:S(2)}) collective-permute-start(bf16[128,1024]{1,0:T(8,128)(2,1)S(1)} %collective-permute-done.1.refs_1_.refs_2_), channel_id=1, source_target_pairs={{0,4},{4,8},{8,12},{12,16},{16,20},{20,24},{24,28},{28,0},{1,5},{5... | collective-permute-start | bytes 786440 | tf_op jit(solution)/shard_map/ppermute | solution.py:89
  17.9 7.9 %collective-permute-start.3 = (bf16[64,1024]{1,0:T(8,128)(2,1)}, bf16[64,1024]{1,0:T(8,128)(2,1)S(1)}, u32[]{:S(2)}, u32[]{:S(2)}) collective-permute-start(bf16[64,1024]{1,0:T(8,128)(2,1)} %get-tuple-element.58), channel_id=1, source_target_pairs={{0,1},{1,2},{2,3},{3,0},{4,5},{5,6},{6,7},{7,4},{8,9},{9,10},{10,1... | collective-permute-start | bytes 393224 | tf_op jit(solution)/shard_map/ppermute | solution.py:89
  19.5 8.0 %collective-permute-start.4 = (bf16[64,1024]{1,0:T(8,128)(2,1)}, bf16[64,1024]{1,0:T(8,128)(2,1)S(1)}, u32[]{:S(2)}, u32[]{:S(2)}) collective-permute-start(bf16[64,1024]{1,0:T(8,128)(2,1)} %get-tuple-element.59), channel_id=1, source_target_pairs={{0,2},{1,3},{2,0},{3,1},{4,6},{5,7},{6,4},{7,5},{8,10},{9,11},{10,... | collective-permute-start | bytes 393224 | tf_op jit(solution)/shard_map/ppermute | solution.py:89
  22.4 5.2 %collective-permute-start.5 = (bf16[64,1024]{1,0:T(8,128)(2,1)}, bf16[64,1024]{1,0:T(8,128)(2,1)S(1)}, u32[]{:S(2)}, u32[]{:S(2)}) collective-permute-start(bf16[64,1024]{1,0:T(8,128)(2,1)} %get-tuple-element.60), channel_id=1, source_target_pairs={{0,3},{1,0},{2,1},{3,2},{4,7},{5,4},{6,5},{7,6},{8,11},{9,8},{10,9... | collective-permute-start | bytes 393224 | tf_op jit(solution)/shard_map/ppermute | solution.py:89
  25.7 56.1 %copy-start.15 = (bf16[64,1024]{1,0:T(8,128)(2,1)}, bf16[64,1024]{1,0:T(8,128)(2,1)S(1)}, u32[]{:S(2)}) copy-start(bf16[64,1024]{1,0:T(8,128)(2,1)S(1)} %collective-permute-done.3.refs_8_) | copy-start | bytes 393220
  27.5 54.3 %copy-start.16 = (bf16[64,1024]{1,0:T(8,128)(2,1)}, bf16[64,1024]{1,0:T(8,128)(2,1)S(1)}, u32[]{:S(2)}) copy-start(bf16[64,1024]{1,0:T(8,128)(2,1)S(1)} %collective-permute-done.4.refs_9_) | copy-start | bytes 393220
  27.6 54.2 %copy-start.17 = (bf16[64,1024]{1,0:T(8,128)(2,1)}, bf16[64,1024]{1,0:T(8,128)(2,1)S(1)}, u32[]{:S(2)}) copy-start(bf16[64,1024]{1,0:T(8,128)(2,1)S(1)} %collective-permute-done.5.refs_10_) | copy-start | bytes 393220
  31.5 11.1 %collective-permute-start.7 = (bf16[128,1024]{1,0:T(8,128)(2,1)}, bf16[128,1024]{1,0:T(8,128)(2,1)S(1)}, u32[]{:S(2)}, u32[]{:S(2)}) collective-permute-start(bf16[128,1024]{1,0:T(8,128)(2,1)} %copy-done.7), channel_id=1, source_target_pairs={{0,28},{4,0},{8,4},{12,8},{16,12},{20,16},{24,20},{28,24},{1,29},{... | collective-permute-start | bytes 786440 | tf_op jit(solution)/shard_map/ppermute | solution.py:89
  35.5 27.4 %collective-permute-start.10 = (bf16[256,1024]{1,0:T(8,128)(2,1)}, bf16[256,1024]{1,0:T(8,128)(2,1)S(1)}, u32[]{:S(2)}, u32[]{:S(2)}) collective-permute-start(bf16[256,1024]{1,0:T(8,128)(2,1)} %get-tuple-element.62), channel_id=1, source_target_pairs={{0,1},{1,2},{2,3},{3,0},{4,5},{5,6},{6,7},{7,4},{8,9},{9,10},{10,1... | collective-permute-start | bytes 1572872 | tf_op jit(solution)/shard_map/ppermute | solution.py:89
  36.5 19.0 %collective-permute-start.8 = (bf16[128,1024]{1,0:T(8,128)(2,1)}, bf16[128,1024]{1,0:T(8,128)(2,1)S(1)}, u32[]{:S(2)}, u32[]{:S(2)}) collective-permute-start(bf16[128,1024]{1,0:T(8,128)(2,1)} %copy-done.8), channel_id=1, source_target_pairs={{0,4},{4,8},{8,12},{12,16},{16,20},{20,24},{24,28},{28,0},{1,5},{5... | collective-permute-start | bytes 786440 | tf_op jit(solution)/shard_map/ppermute | solution.py:89
  42.5 13.0 %copy-start.2 = (bf16[128,1024]{1,0:T(8,128)(2,1)}, bf16[128,1024]{1,0:T(8,128)(2,1)S(1)}, u32[]{:S(2)}) copy-start(bf16[128,1024]{1,0:T(8,128)(2,1)S(1)} %collective-permute-done.7.refs_0_.refs_5_) | copy-start | bytes 786436
  42.5 13.0 %collective-permute-start.9 = (bf16[128,1024]{1,0:T(8,128)(2,1)}, bf16[128,1024]{1,0:T(8,128)(2,1)S(1)}, u32[]{:S(2)}, u32[]{:S(2)}) collective-permute-start(bf16[128,1024]{1,0:T(8,128)(2,1)} %get-tuple-element.68.refs_0_), channel_id=1, source_target_pairs={{0,16},{4,20},{8,24},{12,28},{16,0},{20,4},{24,8},{28,12},{1,17},{... | collective-permute-start | bytes 786440 | tf_op jit(solution)/shard_map/ppermute | solution.py:89
  42.6 22.3 %collective-permute-start.11 = (bf16[256,1024]{1,0:T(8,128)(2,1)}, bf16[256,1024]{1,0:T(8,128)(2,1)S(1)}, u32[]{:S(2)}, u32[]{:S(2)}) collective-permute-start(bf16[256,1024]{1,0:T(8,128)(2,1)} %get-tuple-element.63), channel_id=1, source_target_pairs={{0,2},{1,3},{2,0},{3,1},{4,6},{5,7},{6,4},{7,5},{8,10},{9,11},{10,... | collective-permute-start | bytes 1572872 | tf_op jit(solution)/shard_map/ppermute | solution.py:89
  44.6 25.4 %collective-permute-start.12 = (bf16[256,1024]{1,0:T(8,128)(2,1)}, bf16[256,1024]{1,0:T(8,128)(2,1)S(1)}, u32[]{:S(2)}, u32[]{:S(2)}) collective-permute-start(bf16[256,1024]{1,0:T(8,128)(2,1)} %get-tuple-element.64), channel_id=1, source_target_pairs={{0,3},{1,0},{2,1},{3,2},{4,7},{5,4},{6,5},{7,6},{8,11},{9,8},{10,9... | collective-permute-start | bytes 1572872 | tf_op jit(solution)/shard_map/ppermute | solution.py:89
  59.1 18.6 %collective-permute-start.13 = (bf16[192,1024]{1,0:T(8,128)(2,1)}, bf16[192,1024]{1,0:T(8,128)(2,1)S(1)}, u32[]{:S(2)}, u32[]{:S(2)}) collective-permute-start(bf16[192,1024]{1,0:T(8,128)(2,1)} %get-tuple-element.72), channel_id=1, source_target_pairs={{0,1},{1,2},{2,3},{3,0},{4,5},{5,6},{6,7},{7,4},{8,9},{9,10},{10,1... | collective-permute-start | bytes 1179656 | tf_op jit(solution)/shard_map/ppermute | solution.py:89
  59.7 18.0 %collective-permute-start.14 = (bf16[192,1024]{1,0:T(8,128)(2,1)}, bf16[192,1024]{1,0:T(8,128)(2,1)S(1)}, u32[]{:S(2)}, u32[]{:S(2)}) collective-permute-start(bf16[192,1024]{1,0:T(8,128)(2,1)} %get-tuple-element.73), channel_id=1, source_target_pairs={{0,2},{1,3},{2,0},{3,1},{4,6},{5,7},{6,4},{7,5},{8,10},{9,11},{10,... | collective-permute-start | bytes 1179656 | tf_op jit(solution)/shard_map/ppermute | solution.py:89
  62.9 18.9 %copy-start.9 = (bf16[256,1024]{1,0:T(8,128)(2,1)}, bf16[256,1024]{1,0:T(8,128)(2,1)S(1)}, u32[]{:S(2)}) copy-start(bf16[256,1024]{1,0:T(8,128)(2,1)S(1)} %collective-permute-done.10.refs_11_) | copy-start | bytes 1572868
  62.9 55.8 %copy-start.1 = (s32[32,8]{0,1:T(8,128)S(1)}, s32[32,8]{0,1:T(8,128)}, u32[]{:S(2)}) copy-start(s32[32,8]{0,1:T(8,128)} %param.13) | copy-start | bytes 3076
  62.9 18.9 %collective-permute-start.15 = (bf16[192,1024]{1,0:T(8,128)(2,1)}, bf16[192,1024]{1,0:T(8,128)(2,1)S(1)}, u32[]{:S(2)}, u32[]{:S(2)}) collective-permute-start(bf16[192,1024]{1,0:T(8,128)(2,1)} %get-tuple-element.74), channel_id=1, source_target_pairs={{0,3},{1,0},{2,1},{3,2},{4,7},{5,4},{6,5},{7,6},{8,11},{9,8},{10,9... | collective-permute-start | bytes 1179656 | tf_op jit(solution)/shard_map/ppermute | solution.py:89
  64.9 17.0 %copy-start.10 = (bf16[256,1024]{1,0:T(8,128)(2,1)}, bf16[256,1024]{1,0:T(8,128)(2,1)S(1)}, u32[]{:S(2)}) copy-start(bf16[256,1024]{1,0:T(8,128)(2,1)S(1)} %collective-permute-done.11.refs_12_) | copy-start | bytes 1572868
  70.1 11.8 %copy-start.11 = (bf16[256,1024]{1,0:T(8,128)(2,1)}, bf16[256,1024]{1,0:T(8,128)(2,1)S(1)}, u32[]{:S(2)}) copy-start(bf16[256,1024]{1,0:T(8,128)(2,1)S(1)} %collective-permute-done.12.refs_13_) | copy-start | bytes 1572868
  99.6 14.9 %collective-permute-start.16 = (bf16[128,1024]{1,0:T(8,128)(2,1)}, bf16[128,1024]{1,0:T(8,128)(2,1)S(1)}, u32[]{:S(2)}, u32[]{:S(2)}) collective-permute-start(bf16[128,1024]{1,0:T(8,128)(2,1)} %get-tuple-element.84), channel_id=1, source_target_pairs={{0,3},{1,0},{2,1},{3,2},{4,7},{5,4},{6,5},{7,6},{8,11},{9,8},{10,9... | collective-permute-start | bytes 786440 | tf_op jit(solution)/shard_map/ppermute | solution.py:89
  102.1 12.4 %collective-permute-start.17 = (bf16[128,1024]{1,0:T(8,128)(2,1)}, bf16[128,1024]{1,0:T(8,128)(2,1)S(1)}, u32[]{:S(2)}, u32[]{:S(2)}) collective-permute-start(bf16[128,1024]{1,0:T(8,128)(2,1)} %get-tuple-element.85), channel_id=1, source_target_pairs={{0,2},{1,3},{2,0},{3,1},{4,6},{5,7},{6,4},{7,5},{8,10},{9,11},{10,... | collective-permute-start | bytes 786440 | tf_op jit(solution)/shard_map/ppermute | solution.py:89
  102.1 16.6 %collective-permute-start.18 = (bf16[128,1024]{1,0:T(8,128)(2,1)}, bf16[128,1024]{1,0:T(8,128)(2,1)S(1)}, u32[]{:S(2)}, u32[]{:S(2)}) collective-permute-start(bf16[128,1024]{1,0:T(8,128)(2,1)} %get-tuple-element.86), channel_id=1, source_target_pairs={{0,1},{1,2},{2,3},{3,0},{4,5},{5,6},{6,7},{7,4},{8,9},{9,10},{10,1... | collective-permute-start | bytes 786440 | tf_op jit(solution)/shard_map/ppermute | solution.py:89
  103.1 27.4 %collective-permute-start.19 = (bf16[192,1024]{1,0:T(8,128)(2,1)}, bf16[192,1024]{1,0:T(8,128)(2,1)S(1)}, u32[]{:S(2)}, u32[]{:S(2)}) collective-permute-start(bf16[192,1024]{1,0:T(8,128)(2,1)} %get-tuple-element.91), channel_id=1, source_target_pairs={{0,3},{1,0},{2,1},{3,2},{4,7},{5,4},{6,5},{7,6},{8,11},{9,8},{10,9... | collective-permute-start | bytes 1179656 | tf_op jit(solution)/shard_map/ppermute | solution.py:89
  105.4 28.7 %collective-permute-start.20 = (bf16[192,1024]{1,0:T(8,128)(2,1)}, bf16[192,1024]{1,0:T(8,128)(2,1)S(1)}, u32[]{:S(2)}, u32[]{:S(2)}) collective-permute-start(bf16[192,1024]{1,0:T(8,128)(2,1)} %get-tuple-element.92), channel_id=1, source_target_pairs={{0,2},{1,3},{2,0},{3,1},{4,6},{5,7},{6,4},{7,5},{8,10},{9,11},{10,... | collective-permute-start | bytes 1179656 | tf_op jit(solution)/shard_map/ppermute | solution.py:89
  114.5 19.6 %collective-permute-start.21 = (bf16[192,1024]{1,0:T(8,128)(2,1)}, bf16[192,1024]{1,0:T(8,128)(2,1)S(1)}, u32[]{:S(2)}, u32[]{:S(2)}) collective-permute-start(bf16[192,1024]{1,0:T(8,128)(2,1)} %get-tuple-element.93), channel_id=1, source_target_pairs={{0,1},{1,2},{2,3},{3,0},{4,5},{5,6},{6,7},{7,4},{8,9},{9,10},{10,1... | collective-permute-start | bytes 1179656 | tf_op jit(solution)/shard_map/ppermute | solution.py:89
  120.1 14.0 %copy-start.19 = (bf16[128,1024]{1,0:T(8,128)(2,1)S(1)}, bf16[128,1024]{1,0:T(8,128)(2,1)}, u32[]{:S(2)}) copy-start(bf16[128,1024]{1,0:T(8,128)(2,1)} %get-tuple-element.101) | copy-start | bytes 786436
  120.1 14.0 %copy-start.18 = (bf16[128,1024]{1,0:T(8,128)(2,1)S(1)}, bf16[128,1024]{1,0:T(8,128)(2,1)}, u32[]{:S(2)}) copy-start(bf16[128,1024]{1,0:T(8,128)(2,1)} %get-tuple-element.102) | copy-start | bytes 786436
  121.9 13.4 %collective-permute-start.22 = (bf16[128,1024]{1,0:T(8,128)(2,1)S(1)}, bf16[128,1024]{1,0:T(8,128)(2,1)S(1)}, u32[]{:S(2)}, u32[]{:S(2)}) collective-permute-start(bf16[128,1024]{1,0:T(8,128)(2,1)S(1)} %get-tuple-element.94), channel_id=1, source_target_pairs={{0,4},{4,8},{8,12},{12,16},{16,20},{20,24},{24,28},{28,0},{1,5},{5... | collective-permute-start | bytes 786440 | tf_op jit(solution)/shard_map/ppermute | solution.py:89
  122.2 22.3 %copy-start.23 = (bf16[64,1024]{1,0:T(8,128)(2,1)S(1)}, bf16[64,1024]{1,0:T(8,128)(2,1)}, u32[]{:S(2)}) copy-start(bf16[64,1024]{1,0:T(8,128)(2,1)} %get-tuple-element.97) | copy-start | bytes 393220
  122.2 13.1 %collective-permute-start.23 = (bf16[128,1024]{1,0:T(8,128)(2,1)S(1)}, bf16[128,1024]{1,0:T(8,128)(2,1)S(1)}, u32[]{:S(2)}, u32[]{:S(2)}) collective-permute-start(bf16[128,1024]{1,0:T(8,128)(2,1)S(1)} %get-tuple-element.95), channel_id=1, source_target_pairs={{0,28},{4,0},{8,4},{12,8},{16,12},{20,16},{24,20},{28,24},{1,29},{... | collective-permute-start | bytes 786440 | tf_op jit(solution)/shard_map/ppermute | solution.py:89
  130.5 14.0 %collective-permute-start.27 = (bf16[128,1024]{1,0:T(8,128)(2,1)S(1)}, bf16[128,1024]{1,0:T(8,128)(2,1)S(1)}, u32[]{:S(2)}, u32[]{:S(2)}) collective-permute-start(bf16[128,1024]{1,0:T(8,128)(2,1)S(1)} %copy-done.20), channel_id=1, source_target_pairs={{0,3},{1,0},{2,1},{3,2},{4,7},{5,4},{6,5},{7,6},{8,11},{9,8},{10,9... | collective-permute-start | bytes 786440 | tf_op jit(solution)/shard_map/ppermute | solution.py:89
  134.1 14.1 %collective-permute-start.28 = (bf16[128,1024]{1,0:T(8,128)(2,1)S(1)}, bf16[128,1024]{1,0:T(8,128)(2,1)S(1)}, u32[]{:S(2)}, u32[]{:S(2)}) collective-permute-start(bf16[128,1024]{1,0:T(8,128)(2,1)S(1)} %copy-done.19), channel_id=1, source_target_pairs={{0,2},{1,3},{2,0},{3,1},{4,6},{5,7},{6,4},{7,5},{8,10},{9,11},{10,... | collective-permute-start | bytes 786440 | tf_op jit(solution)/shard_map/ppermute | solution.py:89
  134.1 15.8 %collective-permute-start.29 = (bf16[128,1024]{1,0:T(8,128)(2,1)S(1)}, bf16[128,1024]{1,0:T(8,128)(2,1)S(1)}, u32[]{:S(2)}, u32[]{:S(2)}) collective-permute-start(bf16[128,1024]{1,0:T(8,128)(2,1)S(1)} %copy-done.18), channel_id=1, source_target_pairs={{0,1},{1,2},{2,3},{3,0},{4,5},{5,6},{6,7},{7,4},{8,9},{9,10},{10,1... | collective-permute-start | bytes 786440 | tf_op jit(solution)/shard_map/ppermute | solution.py:89
  137.6 12.3 %collective-permute-start.30 = (bf16[128,1024]{1,0:T(8,128)(2,1)S(1)}, bf16[128,1024]{1,0:T(8,128)(2,1)S(1)}, u32[]{:S(2)}, u32[]{:S(2)}) collective-permute-start(bf16[128,1024]{1,0:T(8,128)(2,1)S(1)} %get-tuple-element.103), channel_id=1, source_target_pairs={{0,4},{4,8},{8,12},{12,16},{16,20},{20,24},{24,28},{28,0},{1,5},{5... | collective-permute-start | bytes 786440 | tf_op jit(solution)/shard_map/ppermute | solution.py:89
  138.5 11.4 %collective-permute-start.31 = (bf16[128,1024]{1,0:T(8,128)(2,1)S(1)}, bf16[128,1024]{1,0:T(8,128)(2,1)S(1)}, u32[]{:S(2)}, u32[]{:S(2)}) collective-permute-start(bf16[128,1024]{1,0:T(8,128)(2,1)S(1)} %get-tuple-element.104), channel_id=1, source_target_pairs={{0,28},{4,0},{8,4},{12,8},{16,12},{20,16},{24,20},{28,24},{1,29},{... | collective-permute-start | bytes 786440 | tf_op jit(solution)/shard_map/ppermute | solution.py:89
  144.5 19.9 %collective-permute-start.24 = (bf16[64,1024]{1,0:T(8,128)(2,1)S(1)}, bf16[64,1024]{1,0:T(8,128)(2,1)S(1)}, u32[]{:S(2)}, u32[]{:S(2)}) collective-permute-start(bf16[64,1024]{1,0:T(8,128)(2,1)S(1)} %copy-done.23), channel_id=1, source_target_pairs={{0,3},{1,0},{2,1},{3,2},{4,7},{5,4},{6,5},{7,6},{8,11},{9,8},{10,9... | collective-permute-start | bytes 393224 | tf_op jit(solution)/shard_map/ppermute | solution.py:89
  148.2 16.2 %copy-start.21 = (bf16[64,1024]{1,0:T(8,128)(2,1)S(1)}, bf16[64,1024]{1,0:T(8,128)(2,1)}, u32[]{:S(2)}) copy-start(bf16[64,1024]{1,0:T(8,128)(2,1)} %get-tuple-element.99) | copy-start | bytes 393220
  148.2 22.4 %collective-permute-start.34 = (bf16[128,1024]{1,0:T(8,128)(2,1)S(1)}, bf16[128,1024]{1,0:T(8,128)(2,1)S(1)}, u32[]{:S(2)}, u32[]{:S(2)}) collective-permute-start(bf16[128,1024]{1,0:T(8,128)(2,1)S(1)} %get-tuple-element.107), channel_id=1, source_target_pairs={{0,16},{4,20},{8,24},{12,28},{16,0},{20,4},{24,8},{28,12},{1,17},{... | collective-permute-start | bytes 786440 | tf_op jit(solution)/shard_map/ppermute | solution.py:89
  151.8 18.9 %collective-permute-start.32 = (bf16[128,1024]{1,0:T(8,128)(2,1)S(1)}, bf16[128,1024]{1,0:T(8,128)(2,1)S(1)}, u32[]{:S(2)}, u32[]{:S(2)}) collective-permute-start(bf16[128,1024]{1,0:T(8,128)(2,1)S(1)} %get-tuple-element.105), channel_id=1, source_target_pairs={{0,4},{4,8},{8,12},{12,16},{16,20},{20,24},{24,28},{28,0},{1,5},{5... | collective-permute-start | bytes 786440 | tf_op jit(solution)/shard_map/ppermute | solution.py:89
  153.9 16.7 %collective-permute-start.33 = (bf16[128,1024]{1,0:T(8,128)(2,1)S(1)}, bf16[128,1024]{1,0:T(8,128)(2,1)S(1)}, u32[]{:S(2)}, u32[]{:S(2)}) collective-permute-start(bf16[128,1024]{1,0:T(8,128)(2,1)S(1)} %get-tuple-element.106), channel_id=1, source_target_pairs={{0,28},{4,0},{8,4},{12,8},{16,12},{20,16},{24,20},{28,24},{1,29},{... | collective-permute-start | bytes 786440 | tf_op jit(solution)/shard_map/ppermute | solution.py:89
  155.1 12.3 %collective-permute-start.25 = (bf16[64,1024]{1,0:T(8,128)(2,1)S(1)}, bf16[64,1024]{1,0:T(8,128)(2,1)S(1)}, u32[]{:S(2)}, u32[]{:S(2)}) collective-permute-start(bf16[64,1024]{1,0:T(8,128)(2,1)S(1)} %copy-done.22), channel_id=1, source_target_pairs={{0,2},{1,3},{2,0},{3,1},{4,6},{5,7},{6,4},{7,5},{8,10},{9,11},{10,... | collective-permute-start | bytes 393224 | tf_op jit(solution)/shard_map/ppermute | solution.py:89
  164.5 6.2 %collective-permute-start.26 = (bf16[64,1024]{1,0:T(8,128)(2,1)S(1)}, bf16[64,1024]{1,0:T(8,128)(2,1)S(1)}, u32[]{:S(2)}, u32[]{:S(2)}) collective-permute-start(bf16[64,1024]{1,0:T(8,128)(2,1)S(1)} %copy-done.21), channel_id=1, source_target_pairs={{0,1},{1,2},{2,3},{3,0},{4,5},{5,6},{6,7},{7,4},{8,9},{9,10},{10,1... | collective-permute-start | bytes 393224 | tf_op jit(solution)/shard_map/ppermute | solution.py:89
  (11 other events, 40.3 us)

commit v2 on v1

--- a/solution.py
+++ b/solution.py
@@ -20,7 +20,7 @@
 YN = 4
 KVW = KV_HEADS * HEAD_DIM
 KEYS = TOK + NEED * BLK
-PAIR = 2 * TOK
+PAIR = 4 * TOK
 SCALE = 1.0 / math.sqrt(HEAD_DIM)
 LOG2E = math.log2(math.e)
 HIDDEN = -1e30
@@ -221,7 +221,7 @@
     k_cols = pl.ds(pl.multiple_of(g * HEAD_DIM, HEAD_DIM), HEAD_DIM)
     v_cols = pl.ds(pl.multiple_of(KVW + g * HEAD_DIM, HEAD_DIM), HEAD_DIM)
     keys, values = kv[:, k_cols], kv[:, v_cols]
-    wide_bias = jnp.concatenate([bias[...]] * 2, axis=1)
+    wide_bias = jnp.concatenate([bias[...]] * 4, axis=1)
 
     def nt(a, b):
         return lax.dot_general(a, b, (((1,), (1,)), ((), ())), preferred_element_type=jnp.float32)
@@ -232,7 +232,7 @@
     def nn(a, b):
         return jnp.dot(a, b, preferred_element_type=jnp.float32)
 
-    for pair in range(GROUP // 2):
+    for pair in range(GROUP // 4):
         rows = slice(pair * PAIR, (pair + 1) * PAIR)
         scores = nt(keys, qs[rows, :]) * (SCALE * LOG2E) + wide_bias
         highest = jnp.max(scores, axis=0, keepdims=True)

time: 173 us -> 172 us (level)
  starting transfers between devices: 71.4 us -> 67 us
  waiting for transfers between devices: 64.1 us -> 67.6 us
    ppermute x35, starting transfers between devices: 71.4 us -> 67 us  [shift(): lax.ppermute(array, axis, [(i, (i + by) % size) for i in range(size)])]
    ppermute x35, waiting for transfers between devices: 64.1 us -> 67.6 us  [shift(): lax.ppermute(array, axis, [(i, (i + by) % size) for i in range(size)])]
  transfers between devices with their start and end apart: 35 -> 35, of which waited for: 15 -> 14; matrix products, arithmetic and copies ran while one was open for 0% -> 0% of each run, Pallas kernels for 5% -> 5%
where the time goes in v2:
time: 172 us; the launch traced here: 173 us
  waiting for transfers between devices  67.6 us (39%)
  starting transfers between devices  67 us (39%)
  Pallas kernels  31.9 us (19%)
  local copies, waits for them, and re-layouts  5 us (3%)
    ppermute x35, waiting for transfers between devices, shift(): lax.ppermute(array, axis, [(i, (i + by) % size) for i in range(size)])  67.6 us
    ppermute x35, starting transfers between devices, shift(): lax.ppermute(array, axis, [(i, (i + by) % size) for i in range(size)])  67 us
    pallas_call x1, Pallas kernels, attend(): pl.pallas_call(attend_body, grid=(KV_HEADS,), out_shape=outs, in_specs=[S...  16.7 us
    pallas_call x4, Pallas kernels, combine(): pl.pallas_call(body, out_shape=shapes, in_specs=[SM] + [ANY] * (4 + len(e...  7.98 us
    pallas_call x2, Pallas kernels, pack(): pl.pallas_call(body, out_shape=[like(count * BLK)] * 3, in_specs=[SM] + [...  5.32 us
    unnamed x48, local copies, waits for them, and re-layouts  5 us
  transfers between devices with their start and end apart: 35, of which 14 were waited for; matrix products, arithmetic and copies ran while one was open for 0% of the time, Pallas kernels for 5%

profile of v2, /device:TPU:4, one launch (start us, length us, event | category | flops | bytes accessed | tf_op | source)
XLA Modules:
  0.0 172.6 jit_solution(2599783512288173475)
XLA Ops:
  0.6 1.9 %join.1 = (bf16[128,1024]{1,0:T(8,128)(2,1)}, bf16[64,1024]{1,0:T(8,128)(2,1)}, bf16[64,1024]{1,0:T(8,128)(2,1)}, bf16[64,1024]{1,0:T(8,128)(2,1)}) custom-call(s32[8,32]{1,0:T(8,128)} %bitcast.1, bf16[128,512]{1,0:T(8,128)(2,1)} %k.1, bf16[128,512]{1,0:T(8,128)(2,1)} %v.1), custom_call_target="tpu_custom_call" | custom-call | tf_op jit(solution)/shard_map/join/pallas_call | solution.py:107
  2.5 5.8 %collective-permute-start = (bf16[128,1024]{1,0:T(8,128)(2,1)}, bf16[128,1024]{1,0:T(8,128)(2,1)S(1)}, u32[]{:S(2)}, u32[]{:S(2)}) collective-permute-start(bf16[128,1024]{1,0:T(8,128)(2,1)} %get-tuple-element.68.refs_0_), channel_id=1, source_target_pairs={{0,28},{4,0},{8,4},{12,8},{16,12},{20,16},{24,20},{28,24},{1,29},{... | collective-permute-start | bytes 786440 | tf_op jit(solution)/shard_map/ppermute | solution.py:89
  8.4 5.9 %collective-permute-done.refs_0_.refs_1_ = bf16[128,1024]{1,0:T(8,128)(2,1)S(1)} collective-permute-done((bf16[128,1024]{1,0:T(8,128)(2,1)}, bf16[128,1024]{1,0:T(8,128)(2,1)S(1)}, u32[]{:S(2)}, u32[]{:S(2)}) %collective-permute-start) | collective-permute-done | bytes 262176 | tf_op jit(solution)/shard_map/ppermute | solution.py:89
  14.3 3.6 %collective-permute-start.2 = (bf16[128,1024]{1,0:T(8,128)(2,1)S(1)}, bf16[128,1024]{1,0:T(8,128)(2,1)S(1)}, u32[]{:S(2)}, u32[]{:S(2)}) collective-permute-start(bf16[128,1024]{1,0:T(8,128)(2,1)S(1)} %collective-permute-done.refs_0_.refs_1_), channel_id=1, source_target_pairs={{0,28},{4,0},{8,4},{12,8},{16,12},{20,16},{24,20},{28,24},{1,29},{... | collective-permute-start | bytes 786440 | tf_op jit(solution)/shard_map/ppermute | solution.py:89
  17.9 1.7 collective-permute-start.3
  19.5 2.9 %collective-permute-start.4 = (bf16[64,1024]{1,0:T(8,128)(2,1)}, bf16[64,1024]{1,0:T(8,128)(2,1)S(1)}, u32[]{:S(2)}, u32[]{:S(2)}) collective-permute-start(bf16[64,1024]{1,0:T(8,128)(2,1)} %get-tuple-element.59), channel_id=1, source_target_pairs={{0,2},{1,3},{2,0},{3,1},{4,6},{5,7},{6,4},{7,5},{8,10},{9,11},{10,... | collective-permute-start | bytes 393224 | tf_op jit(solution)/shard_map/ppermute | solution.py:89
  22.4 1.4 collective-permute-start.5
  23.8 2.0 %collective-permute-done.3.refs_8_ = bf16[64,1024]{1,0:T(8,128)(2,1)S(1)} collective-permute-done((bf16[64,1024]{1,0:T(8,128)(2,1)}, bf16[64,1024]{1,0:T(8,128)(2,1)S(1)}, u32[]{:S(2)}, u32[]{:S(2)}) %collective-permute-start.3) | collective-permute-done | bytes 131104 | tf_op jit(solution)/shard_map/ppermute | solution.py:89
  25.7 1.8 %collective-permute-done.4.refs_9_ = bf16[64,1024]{1,0:T(8,128)(2,1)S(1)} collective-permute-done((bf16[64,1024]{1,0:T(8,128)(2,1)}, bf16[64,1024]{1,0:T(8,128)(2,1)S(1)}, u32[]{:S(2)}, u32[]{:S(2)}) %collective-permute-start.4) | collective-permute-done | bytes 131104 | tf_op jit(solution)/shard_map/ppermute | solution.py:89
  29.1 2.4 %pack.2 = (bf16[256,1024]{1,0:T(8,128)(2,1)}, bf16[256,1024]{1,0:T(8,128)(2,1)}, bf16[256,1024]{1,0:T(8,128)(2,1)}) custom-call(s32[8,32]{1,0:T(8,128)} %bitcast.2, bf16[128,1024]{1,0:T(8,128)(2,1)} %copy-done.5, bf16[128,1024]{1,0:T(8,128)(2,1)} %copy-done.6, bf16[128,1024]{1,0:T(8,128)(2,1)} %copy-done.7, bf16[128,1024]{1,0:T(8,128)(2,1)} %copy-done.8), custom_call_target="tpu_custom_call" | custom-call | tf_op jit(solution)/shard_map/pack/pallas_call | solution.py:78
  31.5 3.9 %collective-permute-start.7 = (bf16[128,1024]{1,0:T(8,128)(2,1)}, bf16[128,1024]{1,0:T(8,128)(2,1)S(1)}, u32[]{:S(2)}, u32[]{:S(2)}) collective-permute-start(bf16[128,1024]{1,0:T(8,128)(2,1)} %copy-done.7), channel_id=1, source_target_pairs={{0,28},{4,0},{8,4},{12,8},{16,12},{20,16},{24,20},{28,24},{1,29},{... | collective-permute-start | bytes 786440 | tf_op jit(solution)/shard_map/ppermute | solution.py:89
  35.4 1.1 collective-permute-start.10
  36.5 6.0 %collective-permute-done.7.refs_0_.refs_5_ = bf16[128,1024]{1,0:T(8,128)(2,1)S(1)} collective-permute-done((bf16[128,1024]{1,0:T(8,128)(2,1)}, bf16[128,1024]{1,0:T(8,128)(2,1)S(1)}, u32[]{:S(2)}, u32[]{:S(2)}) %collective-permute-start.7) | collective-permute-done | bytes 262176 | tf_op jit(solution)/shard_map/ppermute | solution.py:89
  42.5 2.3 %collective-permute-start.11 = (bf16[256,1024]{1,0:T(8,128)(2,1)}, bf16[256,1024]{1,0:T(8,128)(2,1)S(1)}, u32[]{:S(2)}, u32[]{:S(2)}) collective-permute-start(bf16[256,1024]{1,0:T(8,128)(2,1)} %get-tuple-element.63), channel_id=1, source_target_pairs={{0,2},{1,3},{2,0},{3,1},{4,6},{5,7},{6,4},{7,5},{8,10},{9,11},{10,... | collective-permute-start | bytes 1572872 | tf_op jit(solution)/shard_map/ppermute | solution.py:89
  44.7 1.5 collective-permute-start.12
  46.2 9.3 %collective-permute-done.8.refs_1_.refs_6_ = bf16[128,1024]{1,0:T(8,128)(2,1)S(1)} collective-permute-done((bf16[128,1024]{1,0:T(8,128)(2,1)}, bf16[128,1024]{1,0:T(8,128)(2,1)S(1)}, u32[]{:S(2)}, u32[]{:S(2)}) %collective-permute-start.8) | collective-permute-done | bytes 262176 | tf_op jit(solution)/shard_map/ppermute | solution.py:89
  56.9 2.9 %pack.3 = (bf16[192,1024]{1,0:T(8,128)(2,1)}, bf16[192,1024]{1,0:T(8,128)(2,1)}, bf16[192,1024]{1,0:T(8,128)(2,1)}) custom-call(s32[8,32]{1,0:T(8,128)} %bitcast.3, bf16[128,1024]{1,0:T(8,128)(2,1)} %copy-done.2, bf16[128,1024]{1,0:T(8,128)(2,1)} %copy-done.3, bf16[128,1024]{1,0:T(8,128)(2,1)} %copy-done.4), custom_call_target="tpu_custom_call" | custom-call | tf_op jit(solution)/shard_map/pack/pallas_call | solution.py:78
  60.0 3.9 %collective-permute-start.14 = (bf16[192,1024]{1,0:T(8,128)(2,1)}, bf16[192,1024]{1,0:T(8,128)(2,1)S(1)}, u32[]{:S(2)}, u32[]{:S(2)}) collective-permute-start(bf16[192,1024]{1,0:T(8,128)(2,1)} %get-tuple-element.73), channel_id=1, source_target_pairs={{0,2},{1,3},{2,0},{3,1},{4,6},{5,7},{6,4},{7,5},{8,10},{9,11},{10,... | collective-permute-start | bytes 1179656 | tf_op jit(solution)/shard_map/ppermute | solution.py:89
  63.9 1.2 collective-permute-start.15
  65.0 4.3 %collective-permute-done.12.refs_13_ = bf16[256,1024]{1,0:T(8,128)(2,1)S(1)} collective-permute-done((bf16[256,1024]{1,0:T(8,128)(2,1)}, bf16[256,1024]{1,0:T(8,128)(2,1)S(1)}, u32[]{:S(2)}, u32[]{:S(2)}) %collective-permute-start.12) | collective-permute-done | bytes 524320 | tf_op jit(solution)/shard_map/ppermute | solution.py:89
  69.3 9.3 %collective-permute-done.13.refs_14_ = bf16[192,1024]{1,0:T(8,128)(2,1)S(1)} collective-permute-done((bf16[192,1024]{1,0:T(8,128)(2,1)}, bf16[192,1024]{1,0:T(8,128)(2,1)S(1)}, u32[]{:S(2)}, u32[]{:S(2)}) %collective-permute-start.13) | collective-permute-done | bytes 393248 | tf_op jit(solution)/shard_map/ppermute | solution.py:89
  78.6 3.1 %collective-permute-done.15.refs_16_ = bf16[192,1024]{1,0:T(8,128)(2,1)S(1)} collective-permute-done((bf16[192,1024]{1,0:T(8,128)(2,1)}, bf16[192,1024]{1,0:T(8,128)(2,1)S(1)}, u32[]{:S(2)}, u32[]{:S(2)}) %collective-permute-start.15) | collective-permute-done | bytes 393248 | tf_op jit(solution)/shard_map/ppermute | solution.py:89
  81.8 0.7 copy-done.14
  82.6 16.7 %attend.1 = (bf16[128,4096]{1,0:T(8,128)(2,1)}, bf16[128,4096]{1,0:T(8,128)(2,1)}, bf16[640,1024]{1,0:T(8,128)(2,1)}, bf16[128,1024]{1,0:T(8,128)(2,1)}, bf16[12...) custom-call(s32[8,32]{1,0:T(8,128)} %bitcast.4, ...), custom_call_target="tpu_custom_call" | custom-call | tf_op jit(solution)/shard_map/attend/pallas_call | solution.py:284
  99.3 2.5 %collective-permute-start.16 = (bf16[128,1024]{1,0:T(8,128)(2,1)}, bf16[128,1024]{1,0:T(8,128)(2,1)S(1)}, u32[]{:S(2)}, u32[]{:S(2)}) collective-permute-start(bf16[128,1024]{1,0:T(8,128)(2,1)} %get-tuple-element.84), channel_id=1, source_target_pairs={{0,3},{1,0},{2,1},{3,2},{4,7},{5,4},{6,5},{7,6},{8,11},{9,8},{10,9... | collective-permute-start | bytes 786440 | tf_op jit(solution)/shard_map/ppermute | solution.py:89
  101.8 1.0 collective-permute-start.18
  102.8 2.3 %collective-permute-start.19 = (bf16[192,1024]{1,0:T(8,128)(2,1)}, bf16[192,1024]{1,0:T(8,128)(2,1)S(1)}, u32[]{:S(2)}, u32[]{:S(2)}) collective-permute-start(bf16[192,1024]{1,0:T(8,128)(2,1)} %get-tuple-element.91), channel_id=1, source_target_pairs={{0,3},{1,0},{2,1},{3,2},{4,7},{5,4},{6,5},{7,6},{8,11},{9,8},{10,9... | collective-permute-start | bytes 1179656 | tf_op jit(solution)/shard_map/ppermute | solution.py:89
  105.1 2.3 %collective-permute-start.20 = (bf16[192,1024]{1,0:T(8,128)(2,1)}, bf16[192,1024]{1,0:T(8,128)(2,1)S(1)}, u32[]{:S(2)}, u32[]{:S(2)}) collective-permute-start(bf16[192,1024]{1,0:T(8,128)(2,1)} %get-tuple-element.92), channel_id=1, source_target_pairs={{0,2},{1,3},{2,0},{3,1},{4,6},{5,7},{6,4},{7,5},{8,10},{9,11},{10,... | collective-permute-start | bytes 1179656 | tf_op jit(solution)/shard_map/ppermute | solution.py:89
  107.4 6.8 %collective-permute-done.16.refs_0_ = bf16[128,1024]{1,0:T(8,128)(2,1)S(1)} collective-permute-done((bf16[128,1024]{1,0:T(8,128)(2,1)}, bf16[128,1024]{1,0:T(8,128)(2,1)S(1)}, u32[]{:S(2)}, u32[]{:S(2)}) %collective-permute-start.16) | collective-permute-done | bytes 262176 | tf_op jit(solution)/shard_map/ppermute | solution.py:89
  114.2 9.6 %collective-permute-done.18.refs_2_ = bf16[128,1024]{1,0:T(8,128)(2,1)S(1)} collective-permute-done((bf16[128,1024]{1,0:T(8,128)(2,1)}, bf16[128,1024]{1,0:T(8,128)(2,1)S(1)}, u32[]{:S(2)}, u32[]{:S(2)}) %collective-permute-start.18) | collective-permute-done | bytes 262176 | tf_op jit(solution)/shard_map/ppermute | solution.py:89
  123.8 1.3 copy-done
  125.2 1.8 %combine.4 = (bf16[128,1024]{1,0:T(8,128)(2,1)S(1)}, bf16[128,1024]{1,0:T(8,128)(2,1)S(1)}) custom-call(s32[8,32]{1,0:T(8,128)S(1)} %bitcast.5, bf16[640,1024]{1,0:T(8,128)(2,1)S(1)} %copy-done, bf16[128,1024]{1,0:T(8,128)(2,1)S(1)} %collective-permute-done.16.refs_0_, bf16[128,1024]{1,0:T(8,128)(2,1)S(1)} %collective-permute-done.17.refs_1_, ...), custom_call_target="tpu_custom_call" | custom-call | tf_op jit(solution)/shard_map/combine/pallas_call | solution.py:374
  127.1 3.2 %collective-permute-start.23 = (bf16[128,1024]{1,0:T(8,128)(2,1)S(1)}, bf16[128,1024]{1,0:T(8,128)(2,1)S(1)}, u32[]{:S(2)}, u32[]{:S(2)}) collective-permute-start(bf16[128,1024]{1,0:T(8,128)(2,1)S(1)} %get-tuple-element.95), channel_id=1, source_target_pairs={{0,28},{4,0},{8,4},{12,8},{16,12},{20,16},{24,20},{28,24},{1,29},{... | collective-permute-start | bytes 786440 | tf_op jit(solution)/shard_map/ppermute | solution.py:89
  130.3 3.3 %collective-permute-start.27 = (bf16[128,1024]{1,0:T(8,128)(2,1)S(1)}, bf16[128,1024]{1,0:T(8,128)(2,1)S(1)}, u32[]{:S(2)}, u32[]{:S(2)}) collective-permute-start(bf16[128,1024]{1,0:T(8,128)(2,1)S(1)} %copy-done.20), channel_id=1, source_target_pairs={{0,3},{1,0},{2,1},{3,2},{4,7},{5,4},{6,5},{7,6},{8,11},{9,8},{10,9... | collective-permute-start | bytes 786440 | tf_op jit(solution)/shard_map/ppermute | solution.py:89
  133.6 1.2 collective-permute-start.29
  134.8 2.5 %combine.5 = (bf16[128,1024]{1,0:T(8,128)(2,1)S(1)}, bf16[128,1024]{1,0:T(8,128)(2,1)S(1)}, bf16[128,1024]{1,0:T(8,128)(2,1)S(1)}) custom-call(s32[8,32]{1,0:T(8,128)S(1)} %bitcast.6, bf16[640,1024]{1,0:T(8,128)(2,1)S(1)} %copy-done, bf16[192,1024]{1,0:T(8,128)(2,1)S(1)} %collective-permute-done.19.refs_0_, ...), custom_call_target="tpu_custom_call" | custom-call | tf_op jit(solution)/shard_map/combine/pallas_call | solution.py:374
  137.3 2.4 %collective-permute-start.30 = (bf16[128,1024]{1,0:T(8,128)(2,1)S(1)}, bf16[128,1024]{1,0:T(8,128)(2,1)S(1)}, u32[]{:S(2)}, u32[]{:S(2)}) collective-permute-start(bf16[128,1024]{1,0:T(8,128)(2,1)S(1)} %get-tuple-element.103), channel_id=1, source_target_pairs={{0,4},{4,8},{8,12},{12,16},{16,20},{20,24},{24,28},{28,0},{1,5},{5... | collective-permute-start | bytes 786440 | tf_op jit(solution)/shard_map/ppermute | solution.py:89
  139.7 0.9 collective-permute-start.31
  140.6 3.3 %collective-permute-done.27.refs_0_ = bf16[128,1024]{1,0:T(8,128)(2,1)S(1)} collective-permute-done((bf16[128,1024]{1,0:T(8,128)(2,1)S(1)}, bf16[128,1024]{1,0:T(8,128)(2,1)S(1)}, u32[]{:S(2)}, u32[]{:S(2)}) %collective-permute-start.27) | collective-permute-done | bytes 262176 | tf_op jit(solution)/shard_map/ppermute | solution.py:89
  143.9 3.7 %collective-permute-start.24 = (bf16[64,1024]{1,0:T(8,128)(2,1)S(1)}, bf16[64,1024]{1,0:T(8,128)(2,1)S(1)}, u32[]{:S(2)}, u32[]{:S(2)}) collective-permute-start(bf16[64,1024]{1,0:T(8,128)(2,1)S(1)} %copy-done.23), channel_id=1, source_target_pairs={{0,3},{1,0},{2,1},{3,2},{4,7},{5,4},{6,5},{7,6},{8,11},{9,8},{10,9... | collective-permute-start | bytes 393224 | tf_op jit(solution)/shard_map/ppermute | solution.py:89
  147.6 2.0 %collective-permute-start.34 = (bf16[128,1024]{1,0:T(8,128)(2,1)S(1)}, bf16[128,1024]{1,0:T(8,128)(2,1)S(1)}, u32[]{:S(2)}, u32[]{:S(2)}) collective-permute-start(bf16[128,1024]{1,0:T(8,128)(2,1)S(1)} %get-tuple-element.107), channel_id=1, source_target_pairs={{0,16},{4,20},{8,24},{12,28},{16,0},{20,4},{24,8},{28,12},{1,17},{... | collective-permute-start | bytes 786440 | tf_op jit(solution)/shard_map/ppermute | solution.py:89
  149.6 1.6 combine.6
  151.2 2.3 %collective-permute-start.32 = (bf16[128,1024]{1,0:T(8,128)(2,1)S(1)}, bf16[128,1024]{1,0:T(8,128)(2,1)S(1)}, u32[]{:S(2)}, u32[]{:S(2)}) collective-permute-start(bf16[128,1024]{1,0:T(8,128)(2,1)S(1)} %get-tuple-element.105), channel_id=1, source_target_pairs={{0,4},{4,8},{8,12},{12,16},{16,20},{20,24},{24,28},{28,0},{1,5},{5... | collective-permute-start | bytes 786440 | tf_op jit(solution)/shard_map/ppermute | solution.py:89
  153.6 1.7 collective-permute-start.33
  155.2 8.8 %collective-permute-start.25 = (bf16[64,1024]{1,0:T(8,128)(2,1)S(1)}, bf16[64,1024]{1,0:T(8,128)(2,1)S(1)}, u32[]{:S(2)}, u32[]{:S(2)}) collective-permute-start(bf16[64,1024]{1,0:T(8,128)(2,1)S(1)} %copy-done.22), channel_id=1, source_target_pairs={{0,2},{1,3},{2,0},{3,1},{4,6},{5,7},{6,4},{7,5},{8,10},{9,11},{10,... | collective-permute-start | bytes 393224 | tf_op jit(solution)/shard_map/ppermute | solution.py:89
  164.1 2.9 %collective-permute-done.25.refs_1_ = bf16[64,1024]{1,0:T(8,128)(2,1)S(1)} collective-permute-done((bf16[64,1024]{1,0:T(8,128)(2,1)S(1)}, bf16[64,1024]{1,0:T(8,128)(2,1)S(1)}, u32[]{:S(2)}, u32[]{:S(2)}) %collective-permute-start.25) | collective-permute-done | bytes 131104 | tf_op jit(solution)/shard_map/ppermute | solution.py:89
  167.0 3.2 %collective-permute-done.26.refs_2_ = bf16[64,1024]{1,0:T(8,128)(2,1)S(1)} collective-permute-done((bf16[64,1024]{1,0:T(8,128)(2,1)S(1)}, bf16[64,1024]{1,0:T(8,128)(2,1)S(1)}, u32[]{:S(2)}, u32[]{:S(2)}) %collective-permute-start.26) | collective-permute-done | bytes 131104 | tf_op jit(solution)/shard_map/ppermute | solution.py:89
  170.3 2.1 %combine.7 = (bf16[128,512]{1,0:T(8,128)(2,1)}, bf16[128,512]{1,0:T(8,128)(2,1)}) custom-call(s32[8,32]{1,0:T(8,128)S(1)} %bitcast.8, bf16[640,1024]{1,0:T(8,128)(2,1)S(1)} %copy-done, bf16[64,1024]{1,0:T(8,128)(2,1)S(1)} %collective-permute-done.24.refs_0_, bf16[64,1024]{1,0:T(8,128)(2,1)S(1)} %collective-permute-done.25.refs_1_, ...), custom_call_target="tpu_custom_call" | custom-call | tf_op jit(solution)/shard_map/combine/pallas_call | solution.py:374
  (78 shorter events, 3.3 us)
Async XLA Ops:
  2.5 11.7 %collective-permute-start = (bf16[128,1024]{1,0:T(8,128)(2,1)}, bf16[128,1024]{1,0:T(8,128)(2,1)S(1)}, u32[]{:S(2)}, u32[]{:S(2)}) collective-permute-start(bf16[128,1024]{1,0:T(8,128)(2,1)} %get-tuple-element.68.refs_0_), channel_id=1, source_target_pairs={{0,28},{4,0},{8,4},{12,8},{16,12},{20,16},{24,20},{28,24},{1,29},{... | collective-permute-start | bytes 786440 | tf_op jit(solution)/shard_map/ppermute | solution.py:89
  8.4 9.5 %collective-permute-start.1 = (bf16[128,1024]{1,0:T(8,128)(2,1)}, bf16[128,1024]{1,0:T(8,128)(2,1)S(1)}, u32[]{:S(2)}, u32[]{:S(2)}) collective-permute-start(bf16[128,1024]{1,0:T(8,128)(2,1)} %get-tuple-element.68.refs_0_), channel_id=1, source_target_pairs={{0,4},{4,8},{8,12},{12,16},{16,20},{20,24},{24,28},{28,0},{1,5},{5... | collective-permute-start | bytes 786440 | tf_op jit(solution)/shard_map/ppermute | solution.py:89
  14.3 13.3 %copy-start.5 = (bf16[128,1024]{1,0:T(8,128)(2,1)}, bf16[128,1024]{1,0:T(8,128)(2,1)S(1)}, u32[]{:S(2)}) copy-start(bf16[128,1024]{1,0:T(8,128)(2,1)S(1)} %collective-permute-done.refs_0_.refs_1_) | copy-start | bytes 786436
  14.3 13.3 %collective-permute-start.2 = (bf16[128,1024]{1,0:T(8,128)(2,1)S(1)}, bf16[128,1024]{1,0:T(8,128)(2,1)S(1)}, u32[]{:S(2)}, u32[]{:S(2)}) collective-permute-start(bf16[128,1024]{1,0:T(8,128)(2,1)S(1)} %collective-permute-done.refs_0_.refs_1_), channel_id=1, source_target_pairs={{0,28},{4,0},{8,4},{12,8},{16,12},{20,16},{24,20},{28,24},{1,29},{... | collective-permute-start | bytes 786440 | tf_op jit(solution)/shard_map/ppermute | solution.py:89
  17.9 9.8 %copy-start.6 = (bf16[128,1024]{1,0:T(8,128)(2,1)}, bf16[128,1024]{1,0:T(8,128)(2,1)S(1)}, u32[]{:S(2)}) copy-start(bf16[128,1024]{1,0:T(8,128)(2,1)S(1)} %collective-permute-done.1.refs_1_.refs_2_) | copy-start | bytes 786436
  17.9 9.7 %collective-permute-start.6 = (bf16[128,1024]{1,0:T(8,128)(2,1)S(1)}, bf16[128,1024]{1,0:T(8,128)(2,1)S(1)}, u32[]{:S(2)}, u32[]{:S(2)}) collective-permute-start(bf16[128,1024]{1,0:T(8,128)(2,1)S(1)} %collective-permute-done.1.refs_1_.refs_2_), channel_id=1, source_target_pairs={{0,4},{4,8},{8,12},{12,16},{16,20},{20,24},{24,28},{28,0},{1,5},{5... | collective-permute-start | bytes 786440 | tf_op jit(solution)/shard_map/ppermute | solution.py:89
  17.9 7.9 %collective-permute-start.3 = (bf16[64,1024]{1,0:T(8,128)(2,1)}, bf16[64,1024]{1,0:T(8,128)(2,1)S(1)}, u32[]{:S(2)}, u32[]{:S(2)}) collective-permute-start(bf16[64,1024]{1,0:T(8,128)(2,1)} %get-tuple-element.58), channel_id=1, source_target_pairs={{0,1},{1,2},{2,3},{3,0},{4,5},{5,6},{6,7},{7,4},{8,9},{9,10},{10,1... | collective-permute-start | bytes 393224 | tf_op jit(solution)/shard_map/ppermute | solution.py:89
  19.5 8.0 %collective-permute-start.4 = (bf16[64,1024]{1,0:T(8,128)(2,1)}, bf16[64,1024]{1,0:T(8,128)(2,1)S(1)}, u32[]{:S(2)}, u32[]{:S(2)}) collective-permute-start(bf16[64,1024]{1,0:T(8,128)(2,1)} %get-tuple-element.59), channel_id=1, source_target_pairs={{0,2},{1,3},{2,0},{3,1},{4,6},{5,7},{6,4},{7,5},{8,10},{9,11},{10,... | collective-permute-start | bytes 393224 | tf_op jit(solution)/shard_map/ppermute | solution.py:89
  22.4 5.2 %collective-permute-start.5 = (bf16[64,1024]{1,0:T(8,128)(2,1)}, bf16[64,1024]{1,0:T(8,128)(2,1)S(1)}, u32[]{:S(2)}, u32[]{:S(2)}) collective-permute-start(bf16[64,1024]{1,0:T(8,128)(2,1)} %get-tuple-element.60), channel_id=1, source_target_pairs={{0,3},{1,0},{2,1},{3,2},{4,7},{5,4},{6,5},{7,6},{8,11},{9,8},{10,9... | collective-permute-start | bytes 393224 | tf_op jit(solution)/shard_map/ppermute | solution.py:89
  25.7 56.0 %copy-start.15 = (bf16[64,1024]{1,0:T(8,128)(2,1)}, bf16[64,1024]{1,0:T(8,128)(2,1)S(1)}, u32[]{:S(2)}) copy-start(bf16[64,1024]{1,0:T(8,128)(2,1)S(1)} %collective-permute-done.3.refs_8_) | copy-start | bytes 393220
  27.5 54.3 %copy-start.16 = (bf16[64,1024]{1,0:T(8,128)(2,1)}, bf16[64,1024]{1,0:T(8,128)(2,1)S(1)}, u32[]{:S(2)}) copy-start(bf16[64,1024]{1,0:T(8,128)(2,1)S(1)} %collective-permute-done.4.refs_9_) | copy-start | bytes 393220
  27.6 54.2 %copy-start.17 = (bf16[64,1024]{1,0:T(8,128)(2,1)}, bf16[64,1024]{1,0:T(8,128)(2,1)S(1)}, u32[]{:S(2)}) copy-start(bf16[64,1024]{1,0:T(8,128)(2,1)S(1)} %collective-permute-done.5.refs_10_) | copy-start | bytes 393220
  31.5 11.0 %collective-permute-start.7 = (bf16[128,1024]{1,0:T(8,128)(2,1)}, bf16[128,1024]{1,0:T(8,128)(2,1)S(1)}, u32[]{:S(2)}, u32[]{:S(2)}) collective-permute-start(bf16[128,1024]{1,0:T(8,128)(2,1)} %copy-done.7), channel_id=1, source_target_pairs={{0,28},{4,0},{8,4},{12,8},{16,12},{20,16},{24,20},{28,24},{1,29},{... | collective-permute-start | bytes 786440 | tf_op jit(solution)/shard_map/ppermute | solution.py:89
  35.4 28.5 %collective-permute-start.10 = (bf16[256,1024]{1,0:T(8,128)(2,1)}, bf16[256,1024]{1,0:T(8,128)(2,1)S(1)}, u32[]{:S(2)}, u32[]{:S(2)}) collective-permute-start(bf16[256,1024]{1,0:T(8,128)(2,1)} %get-tuple-element.62), channel_id=1, source_target_pairs={{0,1},{1,2},{2,3},{3,0},{4,5},{5,6},{6,7},{7,4},{8,9},{9,10},{10,1... | collective-permute-start | bytes 1572872 | tf_op jit(solution)/shard_map/ppermute | solution.py:89
  36.5 19.0 %collective-permute-start.8 = (bf16[128,1024]{1,0:T(8,128)(2,1)}, bf16[128,1024]{1,0:T(8,128)(2,1)S(1)}, u32[]{:S(2)}, u32[]{:S(2)}) collective-permute-start(bf16[128,1024]{1,0:T(8,128)(2,1)} %copy-done.8), channel_id=1, source_target_pairs={{0,4},{4,8},{8,12},{12,16},{16,20},{20,24},{24,28},{28,0},{1,5},{5... | collective-permute-start | bytes 786440 | tf_op jit(solution)/shard_map/ppermute | solution.py:89
  42.5 13.1 %copy-start.2 = (bf16[128,1024]{1,0:T(8,128)(2,1)}, bf16[128,1024]{1,0:T(8,128)(2,1)S(1)}, u32[]{:S(2)}) copy-start(bf16[128,1024]{1,0:T(8,128)(2,1)S(1)} %collective-permute-done.7.refs_0_.refs_5_) | copy-start | bytes 786436
  42.5 13.1 %collective-permute-start.9 = (bf16[128,1024]{1,0:T(8,128)(2,1)}, bf16[128,1024]{1,0:T(8,128)(2,1)S(1)}, u32[]{:S(2)}, u32[]{:S(2)}) collective-permute-start(bf16[128,1024]{1,0:T(8,128)(2,1)} %get-tuple-element.68.refs_0_), channel_id=1, source_target_pairs={{0,16},{4,20},{8,24},{12,28},{16,0},{20,4},{24,8},{28,12},{1,17},{... | collective-permute-start | bytes 786440 | tf_op jit(solution)/shard_map/ppermute | solution.py:89
  42.5 22.6 %collective-permute-start.11 = (bf16[256,1024]{1,0:T(8,128)(2,1)}, bf16[256,1024]{1,0:T(8,128)(2,1)S(1)}, u32[]{:S(2)}, u32[]{:S(2)}) collective-permute-start(bf16[256,1024]{1,0:T(8,128)(2,1)} %get-tuple-element.63), channel_id=1, source_target_pairs={{0,2},{1,3},{2,0},{3,1},{4,6},{5,7},{6,4},{7,5},{8,10},{9,11},{10,... | collective-permute-start | bytes 1572872 | tf_op jit(solution)/shard_map/ppermute | solution.py:89
  44.7 24.6 %collective-permute-start.12 = (bf16[256,1024]{1,0:T(8,128)(2,1)}, bf16[256,1024]{1,0:T(8,128)(2,1)S(1)}, u32[]{:S(2)}, u32[]{:S(2)}) collective-permute-start(bf16[256,1024]{1,0:T(8,128)(2,1)} %get-tuple-element.64), channel_id=1, source_target_pairs={{0,3},{1,0},{2,1},{3,2},{4,7},{5,4},{6,5},{7,6},{8,11},{9,8},{10,9... | collective-permute-start | bytes 1572872 | tf_op jit(solution)/shard_map/ppermute | solution.py:89
  59.9 18.7 %collective-permute-start.13 = (bf16[192,1024]{1,0:T(8,128)(2,1)}, bf16[192,1024]{1,0:T(8,128)(2,1)S(1)}, u32[]{:S(2)}, u32[]{:S(2)}) collective-permute-start(bf16[192,1024]{1,0:T(8,128)(2,1)} %get-tuple-element.72), channel_id=1, source_target_pairs={{0,1},{1,2},{2,3},{3,0},{4,5},{5,6},{6,7},{7,4},{8,9},{9,10},{10,1... | collective-permute-start | bytes 1179656 | tf_op jit(solution)/shard_map/ppermute | solution.py:89
  60.0 18.6 %collective-permute-start.14 = (bf16[192,1024]{1,0:T(8,128)(2,1)}, bf16[192,1024]{1,0:T(8,128)(2,1)S(1)}, u32[]{:S(2)}, u32[]{:S(2)}) collective-permute-start(bf16[192,1024]{1,0:T(8,128)(2,1)} %get-tuple-element.73), channel_id=1, source_target_pairs={{0,2},{1,3},{2,0},{3,1},{4,6},{5,7},{6,4},{7,5},{8,10},{9,11},{10,... | collective-permute-start | bytes 1179656 | tf_op jit(solution)/shard_map/ppermute | solution.py:89
  63.9 17.9 %copy-start.9 = (bf16[256,1024]{1,0:T(8,128)(2,1)}, bf16[256,1024]{1,0:T(8,128)(2,1)S(1)}, u32[]{:S(2)}) copy-start(bf16[256,1024]{1,0:T(8,128)(2,1)S(1)} %collective-permute-done.10.refs_11_) | copy-start | bytes 1572868
  63.9 60.0 %copy-start.1 = (s32[32,8]{0,1:T(8,128)S(1)}, s32[32,8]{0,1:T(8,128)}, u32[]{:S(2)}) copy-start(s32[32,8]{0,1:T(8,128)} %param.13) | copy-start | bytes 3076
  63.9 17.9 %collective-permute-start.15 = (bf16[192,1024]{1,0:T(8,128)(2,1)}, bf16[192,1024]{1,0:T(8,128)(2,1)S(1)}, u32[]{:S(2)}, u32[]{:S(2)}) collective-permute-start(bf16[192,1024]{1,0:T(8,128)(2,1)} %get-tuple-element.74), channel_id=1, source_target_pairs={{0,3},{1,0},{2,1},{3,2},{4,7},{5,4},{6,5},{7,6},{8,11},{9,8},{10,9... | collective-permute-start | bytes 1179656 | tf_op jit(solution)/shard_map/ppermute | solution.py:89
  65.0 16.8 %copy-start.10 = (bf16[256,1024]{1,0:T(8,128)(2,1)}, bf16[256,1024]{1,0:T(8,128)(2,1)S(1)}, u32[]{:S(2)}) copy-start(bf16[256,1024]{1,0:T(8,128)(2,1)S(1)} %collective-permute-done.11.refs_12_) | copy-start | bytes 1572868
  69.3 12.5 %copy-start.11 = (bf16[256,1024]{1,0:T(8,128)(2,1)}, bf16[256,1024]{1,0:T(8,128)(2,1)S(1)}, u32[]{:S(2)}) copy-start(bf16[256,1024]{1,0:T(8,128)(2,1)S(1)} %collective-permute-done.12.refs_13_) | copy-start | bytes 1572868
  99.3 14.9 %collective-permute-start.16 = (bf16[128,1024]{1,0:T(8,128)(2,1)}, bf16[128,1024]{1,0:T(8,128)(2,1)S(1)}, u32[]{:S(2)}, u32[]{:S(2)}) collective-permute-start(bf16[128,1024]{1,0:T(8,128)(2,1)} %get-tuple-element.84), channel_id=1, source_target_pairs={{0,3},{1,0},{2,1},{3,2},{4,7},{5,4},{6,5},{7,6},{8,11},{9,8},{10,9... | collective-permute-start | bytes 786440 | tf_op jit(solution)/shard_map/ppermute | solution.py:89
  101.8 12.4 %collective-permute-start.17 = (bf16[128,1024]{1,0:T(8,128)(2,1)}, bf16[128,1024]{1,0:T(8,128)(2,1)S(1)}, u32[]{:S(2)}, u32[]{:S(2)}) collective-permute-start(bf16[128,1024]{1,0:T(8,128)(2,1)} %get-tuple-element.85), channel_id=1, source_target_pairs={{0,2},{1,3},{2,0},{3,1},{4,6},{5,7},{6,4},{7,5},{8,10},{9,11},{10,... | collective-permute-start | bytes 786440 | tf_op jit(solution)/shard_map/ppermute | solution.py:89
  101.8 22.0 %collective-permute-start.18 = (bf16[128,1024]{1,0:T(8,128)(2,1)}, bf16[128,1024]{1,0:T(8,128)(2,1)S(1)}, u32[]{:S(2)}, u32[]{:S(2)}) collective-permute-start(bf16[128,1024]{1,0:T(8,128)(2,1)} %get-tuple-element.86), channel_id=1, source_target_pairs={{0,1},{1,2},{2,3},{3,0},{4,5},{5,6},{6,7},{7,4},{8,9},{9,10},{10,1... | collective-permute-start | bytes 786440 | tf_op jit(solution)/shard_map/ppermute | solution.py:89
  102.8 27.5 %collective-permute-start.19 = (bf16[192,1024]{1,0:T(8,128)(2,1)}, bf16[192,1024]{1,0:T(8,128)(2,1)S(1)}, u32[]{:S(2)}, u32[]{:S(2)}) collective-permute-start(bf16[192,1024]{1,0:T(8,128)(2,1)} %get-tuple-element.91), channel_id=1, source_target_pairs={{0,3},{1,0},{2,1},{3,2},{4,7},{5,4},{6,5},{7,6},{8,11},{9,8},{10,9... | collective-permute-start | bytes 1179656 | tf_op jit(solution)/shard_map/ppermute | solution.py:89
  105.1 28.6 %collective-permute-start.20 = (bf16[192,1024]{1,0:T(8,128)(2,1)}, bf16[192,1024]{1,0:T(8,128)(2,1)S(1)}, u32[]{:S(2)}, u32[]{:S(2)}) collective-permute-start(bf16[192,1024]{1,0:T(8,128)(2,1)} %get-tuple-element.92), channel_id=1, source_target_pairs={{0,2},{1,3},{2,0},{3,1},{4,6},{5,7},{6,4},{7,5},{8,10},{9,11},{10,... | collective-permute-start | bytes 1179656 | tf_op jit(solution)/shard_map/ppermute | solution.py:89
  114.2 19.4 %collective-permute-start.21 = (bf16[192,1024]{1,0:T(8,128)(2,1)}, bf16[192,1024]{1,0:T(8,128)(2,1)S(1)}, u32[]{:S(2)}, u32[]{:S(2)}) collective-permute-start(bf16[192,1024]{1,0:T(8,128)(2,1)} %get-tuple-element.93), channel_id=1, source_target_pairs={{0,1},{1,2},{2,3},{3,0},{4,5},{5,6},{6,7},{7,4},{8,9},{9,10},{10,1... | collective-permute-start | bytes 1179656 | tf_op jit(solution)/shard_map/ppermute | solution.py:89
  125.2 8.5 %copy-start.18 = (bf16[128,1024]{1,0:T(8,128)(2,1)S(1)}, bf16[128,1024]{1,0:T(8,128)(2,1)}, u32[]{:S(2)}) copy-start(bf16[128,1024]{1,0:T(8,128)(2,1)} %get-tuple-element.102) | copy-start | bytes 786436
  127.0 7.9 %collective-permute-start.22 = (bf16[128,1024]{1,0:T(8,128)(2,1)S(1)}, bf16[128,1024]{1,0:T(8,128)(2,1)S(1)}, u32[]{:S(2)}, u32[]{:S(2)}) collective-permute-start(bf16[128,1024]{1,0:T(8,128)(2,1)S(1)} %get-tuple-element.94), channel_id=1, source_target_pairs={{0,4},{4,8},{8,12},{12,16},{16,20},{20,24},{24,28},{28,0},{1,5},{5... | collective-permute-start | bytes 786440 | tf_op jit(solution)/shard_map/ppermute | solution.py:89
  127.0 16.9 %copy-start.23 = (bf16[64,1024]{1,0:T(8,128)(2,1)S(1)}, bf16[64,1024]{1,0:T(8,128)(2,1)}, u32[]{:S(2)}) copy-start(bf16[64,1024]{1,0:T(8,128)(2,1)} %get-tuple-element.97) | copy-start | bytes 393220
  127.1 7.8 %collective-permute-start.23 = (bf16[128,1024]{1,0:T(8,128)(2,1)S(1)}, bf16[128,1024]{1,0:T(8,128)(2,1)S(1)}, u32[]{:S(2)}, u32[]{:S(2)}) collective-permute-start(bf16[128,1024]{1,0:T(8,128)(2,1)S(1)} %get-tuple-element.95), channel_id=1, source_target_pairs={{0,28},{4,0},{8,4},{12,8},{16,12},{20,16},{24,20},{28,24},{1,29},{... | collective-permute-start | bytes 786440 | tf_op jit(solution)/shard_map/ppermute | solution.py:89
  130.3 13.6 %collective-permute-start.27 = (bf16[128,1024]{1,0:T(8,128)(2,1)S(1)}, bf16[128,1024]{1,0:T(8,128)(2,1)S(1)}, u32[]{:S(2)}, u32[]{:S(2)}) collective-permute-start(bf16[128,1024]{1,0:T(8,128)(2,1)S(1)} %copy-done.20), channel_id=1, source_target_pairs={{0,3},{1,0},{2,1},{3,2},{4,7},{5,4},{6,5},{7,6},{8,11},{9,8},{10,9... | collective-permute-start | bytes 786440 | tf_op jit(solution)/shard_map/ppermute | solution.py:89
  133.6 14.0 %collective-permute-start.28 = (bf16[128,1024]{1,0:T(8,128)(2,1)S(1)}, bf16[128,1024]{1,0:T(8,128)(2,1)S(1)}, u32[]{:S(2)}, u32[]{:S(2)}) collective-permute-start(bf16[128,1024]{1,0:T(8,128)(2,1)S(1)} %copy-done.19), channel_id=1, source_target_pairs={{0,2},{1,3},{2,0},{3,1},{4,6},{5,7},{6,4},{7,5},{8,10},{9,11},{10,... | collective-permute-start | bytes 786440 | tf_op jit(solution)/shard_map/ppermute | solution.py:89
  133.6 16.0 %collective-permute-start.29 = (bf16[128,1024]{1,0:T(8,128)(2,1)S(1)}, bf16[128,1024]{1,0:T(8,128)(2,1)S(1)}, u32[]{:S(2)}, u32[]{:S(2)}) collective-permute-start(bf16[128,1024]{1,0:T(8,128)(2,1)S(1)} %copy-done.18), channel_id=1, source_target_pairs={{0,1},{1,2},{2,3},{3,0},{4,5},{5,6},{6,7},{7,4},{8,9},{9,10},{10,1... | collective-permute-start | bytes 786440 | tf_op jit(solution)/shard_map/ppermute | solution.py:89
  137.3 12.3 %collective-permute-start.30 = (bf16[128,1024]{1,0:T(8,128)(2,1)S(1)}, bf16[128,1024]{1,0:T(8,128)(2,1)S(1)}, u32[]{:S(2)}, u32[]{:S(2)}) collective-permute-start(bf16[128,1024]{1,0:T(8,128)(2,1)S(1)} %get-tuple-element.103), channel_id=1, source_target_pairs={{0,4},{4,8},{8,12},{12,16},{16,20},{20,24},{24,28},{28,0},{1,5},{5... | collective-permute-start | bytes 786440 | tf_op jit(solution)/shard_map/ppermute | solution.py:89
  139.7 9.9 %collective-permute-start.31 = (bf16[128,1024]{1,0:T(8,128)(2,1)S(1)}, bf16[128,1024]{1,0:T(8,128)(2,1)S(1)}, u32[]{:S(2)}, u32[]{:S(2)}) collective-permute-start(bf16[128,1024]{1,0:T(8,128)(2,1)S(1)} %get-tuple-element.104), channel_id=1, source_target_pairs={{0,28},{4,0},{8,4},{12,8},{16,12},{20,16},{24,20},{28,24},{1,29},{... | collective-permute-start | bytes 786440 | tf_op jit(solution)/shard_map/ppermute | solution.py:89
  143.9 20.2 %collective-permute-start.24 = (bf16[64,1024]{1,0:T(8,128)(2,1)S(1)}, bf16[64,1024]{1,0:T(8,128)(2,1)S(1)}, u32[]{:S(2)}, u32[]{:S(2)}) collective-permute-start(bf16[64,1024]{1,0:T(8,128)(2,1)S(1)} %copy-done.23), channel_id=1, source_target_pairs={{0,3},{1,0},{2,1},{3,2},{4,7},{5,4},{6,5},{7,6},{8,11},{9,8},{10,9... | collective-permute-start | bytes 393224 | tf_op jit(solution)/shard_map/ppermute | solution.py:89
  147.6 16.5 %copy-start.21 = (bf16[64,1024]{1,0:T(8,128)(2,1)S(1)}, bf16[64,1024]{1,0:T(8,128)(2,1)}, u32[]{:S(2)}) copy-start(bf16[64,1024]{1,0:T(8,128)(2,1)} %get-tuple-element.99) | copy-start | bytes 393220
  147.6 22.6 %collective-permute-start.34 = (bf16[128,1024]{1,0:T(8,128)(2,1)S(1)}, bf16[128,1024]{1,0:T(8,128)(2,1)S(1)}, u32[]{:S(2)}, u32[]{:S(2)}) collective-permute-start(bf16[128,1024]{1,0:T(8,128)(2,1)S(1)} %get-tuple-element.107), channel_id=1, source_target_pairs={{0,16},{4,20},{8,24},{12,28},{16,0},{20,4},{24,8},{28,12},{1,17},{... | collective-permute-start | bytes 786440 | tf_op jit(solution)/shard_map/ppermute | solution.py:89
  151.2 19.0 %collective-permute-start.32 = (bf16[128,1024]{1,0:T(8,128)(2,1)S(1)}, bf16[128,1024]{1,0:T(8,128)(2,1)S(1)}, u32[]{:S(2)}, u32[]{:S(2)}) collective-permute-start(bf16[128,1024]{1,0:T(8,128)(2,1)S(1)} %get-tuple-element.105), channel_id=1, source_target_pairs={{0,4},{4,8},{8,12},{12,16},{16,20},{20,24},{24,28},{28,0},{1,5},{5... | collective-permute-start | bytes 786440 | tf_op jit(solution)/shard_map/ppermute | solution.py:89
  153.6 16.7 %collective-permute-start.33 = (bf16[128,1024]{1,0:T(8,128)(2,1)S(1)}, bf16[128,1024]{1,0:T(8,128)(2,1)S(1)}, u32[]{:S(2)}, u32[]{:S(2)}) collective-permute-start(bf16[128,1024]{1,0:T(8,128)(2,1)S(1)} %get-tuple-element.106), channel_id=1, source_target_pairs={{0,28},{4,0},{8,4},{12,8},{16,12},{20,16},{24,20},{28,24},{1,29},{... | collective-permute-start | bytes 786440 | tf_op jit(solution)/shard_map/ppermute | solution.py:89
  155.2 11.8 %collective-permute-start.25 = (bf16[64,1024]{1,0:T(8,128)(2,1)S(1)}, bf16[64,1024]{1,0:T(8,128)(2,1)S(1)}, u32[]{:S(2)}, u32[]{:S(2)}) collective-permute-start(bf16[64,1024]{1,0:T(8,128)(2,1)S(1)} %copy-done.22), channel_id=1, source_target_pairs={{0,2},{1,3},{2,0},{3,1},{4,6},{5,7},{6,4},{7,5},{8,10},{9,11},{10,... | collective-permute-start | bytes 393224 | tf_op jit(solution)/shard_map/ppermute | solution.py:89
  164.1 6.2 %collective-permute-start.26 = (bf16[64,1024]{1,0:T(8,128)(2,1)S(1)}, bf16[64,1024]{1,0:T(8,128)(2,1)S(1)}, u32[]{:S(2)}, u32[]{:S(2)}) collective-permute-start(bf16[64,1024]{1,0:T(8,128)(2,1)S(1)} %copy-done.21), channel_id=1, source_target_pairs={{0,1},{1,2},{2,3},{3,0},{4,5},{5,6},{6,7},{7,4},{8,9},{9,10},{10,1... | collective-permute-start | bytes 393224 | tf_op jit(solution)/shard_map/ppermute | solution.py:89
  (11 other events, 32.6 us)
